TPU v7x, 128 devices: a whole 4x4x4 slice. The times are simulated.
128 devices in a mesh: row: 16 (over y, x), col: 8 (over z, core).
Axes of the slice: x: 4, y: 4, z: 4, core: 2. Of those that a mesh axis runs over, the one named last changes fastest.
Arguments:
- front_first: float32 [16, 4, 128, 8, 8, 128], P('row', None, None, 'col'), as said below
- front_second: float32 [16, 4, 128, 8, 8, 128], P('row', None, None, 'col'), as said below
- front_third: float32 [16, 4, 128, 8, 8, 128], P('row', None, None, 'col'), as said below
- map_second: int32 [60], replicated, may hold values from 0 to 63, as said below
- map_third: int32 [60], replicated, may hold values from 0 to 63, as said below
Outputs:
- lower_first: float32 [16, 4, 128, 512], P('row')
- lower_second: float32 [16, 4, 128, 512], P('row')
- lower_third: float32 [16, 4, 128, 512], P('row')
- schur_third: float32 [16, 4, 128, 8, 8, 128], P('row', None, None, 'col')
Inputs may be any that keep to these rules, and one draw needn't show every extreme that they name: `map_second`: strictly increasing; the first entry is 0 and the last is 63. `map_third`: strictly increasing; the first entry is 0 and the last is 63. `front_first`: symmetric positive definite. `front_second`: symmetric positive definite. `front_third`: symmetric positive definite.
All inputs are finite; a program needn't handle non-finite values.
Results may differ from a plain program's by a relative error of at most 0.00012.
Values sent between devices are 32-bit elements; how exact they have to be, the bound alone decides.
No kernel may reach another device: no remote copies, remote signals or barrier semaphores. Data moves between devices by JAX's collectives and lax.ppermute only.
A program may use at most 128 MiB of HBM per device.

v0:
```python
import jax
import jax.numpy as jnp
from jax import lax
from jax.experimental import pallas as pl
from jax.experimental.pallas import tpu as pltpu
from jax.sharding import PartitionSpec as P

TILE = 128
PIVOTS = 512
BLOCKS = 64
ROWS = 16
COLS = 8
TR = 4
TC = 8
MAXD = 4
F32 = jnp.float32
HI = lax.Precision.HIGHEST
BOTH = ("row", "col")


def full(x):
    return jnp.broadcast_to(x, (8, 128))


def base128(tiles, inv):
    sub = lax.broadcasted_iota(jnp.int32, (8, 128), 0)
    n = len(tiles)
    for b in range(n):
        c0 = 8 * b
        rows = tiles[b]
        cols = [full(rows[:, c0 + c : c0 + c + 1]) for c in range(8)]
        e = [[full(cols[c][r : r + 1, :]) for c in range(r + 1)] for r in range(8)]
        low = [[None] * 8 for _ in range(8)]
        s = [None] * 8
        for j in range(8):
            s[j] = lax.rsqrt(e[j][j])
            for i in range(j + 1, 8):
                low[i][j] = e[i][j] * s[j]
            for i in range(j + 1, 8):
                for k in range(j + 1, i + 1):
                    e[i][k] = e[i][k] - low[i][j] * low[k][j]
        w = [[None] * 8 for _ in range(8)]
        for k in range(8):
            w[k][k] = s[k]
            for i in range(k + 1, 8):
                acc = low[i][k] * w[k][k]
                for m in range(k + 1, i):
                    acc = acc + low[i][m] * w[m][k]
                w[i][k] = -(acc * s[i])
        wcol = []
        for k in range(8):
            v = w[7][k]
            for i in range(6, k - 1, -1):
                v = jnp.where(sub == i, w[i][k], v)
            if k > 0:
                v = jnp.where(sub < k, 0.0, v)
            wcol.append(v)

        def apply(x):
            acc = wcol[0] * full(x[0:1, :])
            for k in range(1, 8):
                acc = acc + wcol[k] * full(x[k : k + 1, :])
            return acc

        upper = apply(rows)
        inv[b] = apply(inv[b])
        if b == n - 1:
            break

        def weighted(x):
            parts = [full(x[i : i + 1, :]) for i in range(8)]
            out = []
            for k in range(8):
                acc = w[k][k] * parts[k]
                for i in range(k + 1, 8):
                    acc = acc + w[i][k] * parts[i]
                out.append(acc)
            return out

        zt = weighted(upper)
        zv = weighted(inv[b])
        for r in range(b + 1, n):
            t = tiles[r]
            v = inv[r]
            for k in range(8):
                c = full(tiles[r][:, c0 + k : c0 + k + 1])
                t = t - c * zt[k]
                v = v - c * zv[k]
            tiles[r] = t
            inv[r] = v
    return inv


def kdot(a, b, dims=(((1,), (0,)), ((), ()))):
    return lax.dot_general(a, b, dims, precision=HI, preferred_element_type=F32)


TN = (((0,), (0,)), ((), ()))


def chol_kernel(d_ref, w_ref, a_ref, wk_ref):
    a_ref[...] = d_ref[...]
    w_ref[...] = jnp.zeros((PIVOTS, PIVOTS), F32)
    ri = lax.broadcasted_iota(jnp.int32, (8, 128), 0)
    ci = lax.broadcasted_iota(jnp.int32, (8, 128), 1)

    def body(kb, carry):
        o = pl.multiple_of(kb * 128, 128)
        tiles = [a_ref[pl.ds(o + 8 * r, 8), pl.ds(o, 128)] for r in range(16)]
        inv = [jnp.where(ri + 8 * r == ci, 1.0, 0.0).astype(F32) for r in range(16)]
        inv = base128(tiles, inv)
        for r in range(16):
            wk_ref[8 * r : 8 * r + 8, :] = inv[r]
        for kk in range(4):

            @pl.when(kb == kk)
            def _(kk=kk):
                k0 = kk * 128
                k1 = k0 + 128
                wk = wk_ref[...]
                if kk > 0:
                    w_ref[k0:k1, :k0] = kdot(wk, w_ref[k0:k1, :k0])
                w_ref[k0:k1, k0:k1] = wk
                if kk < 3:
                    u = kdot(wk, a_ref[k0:k1, k1:])
                    a_ref[k1:, k1:] = a_ref[k1:, k1:] - kdot(u, u, TN)
                    w_ref[k1:, :k1] = w_ref[k1:, :k1] - kdot(u, w_ref[k0:k1, :k1], TN)

        return carry

    lax.fori_loop(0, 4, body, 0)


def inverse_factor(d):
    return pl.pallas_call(
        chol_kernel,
        out_shape=jax.ShapeDtypeStruct((PIVOTS, PIVOTS), F32),
        scratch_shapes=[pltpu.VMEM((PIVOTS, PIVOTS), F32), pltpu.VMEM((128, 128), F32)],
        cost_estimate=pl.CostEstimate(
            flops=25_000_000_000, transcendentals=512, bytes_accessed=2_000_000
        ),
        compiler_params=pltpu.CompilerParams(vmem_limit_bytes=32 << 20),
    )(d)


def panel_kernel(c1_ref, c2_ref, k_ref, r1_ref, r2_ref, r3_ref, g_ref, h_ref, s_ref):
    def row(i, j, t, c):
        return k_ref[i, j, pl.ds(t * 4 + c, 1), :]

    def first(p, carry):
        t = p // ROWS
        i = p % ROWS
        for q in range(4):
            r1_ref[p, q : q + 1, :] = row(i, q, t, 0)
        cp = c1_ref[p]
        cc = jnp.maximum(cp, 0)
        tt = cc // ROWS
        ii = cc % ROWS
        for q in range(8):
            cq = c1_ref[q]
            qq = jnp.maximum(cq, 0)
            got = row(ii, qq % COLS, tt, qq // COLS)
            got = jnp.where((cp >= 0) & (cq >= 0), got, 0.0)
            val = row(i, q, t, 2) + got
            s_ref[p, q : q + 1, :] = val
            if q < 4:
                r2_ref[p, q : q + 1, :] = val
        return carry

    lax.fori_loop(0, BLOCKS, first, 0)

    def second(p, carry):
        t = p // ROWS
        i = p % ROWS
        cp = c2_ref[p]
        cc = jnp.maximum(cp, 0)
        for q in range(4):
            cq = c2_ref[q]
            qq = jnp.maximum(cq, 0)
            got = s_ref[cc, pl.ds(qq, 1), :]
            got = jnp.where((cp >= 0) & (cq >= 0), got, 0.0)
            r3_ref[p, q : q + 1, :] = row(i, q, t, 3) + got
        c12 = c1_ref[cc]
        j = p % COLS
        s = p // COLS
        h_ref[j, 0, s] = jnp.where(
            (cp >= 0) & (c12 >= 0), r1_ref[jnp.maximum(c12, 0)], 0.0
        )
        h_ref[j, 1, s] = jnp.where(cp >= 0, r2_ref[cc], 0.0)
        h_ref[j, 2, s] = r3_ref[p]
        return carry

    lax.fori_loop(0, BLOCKS, second, 0)
    g_ref[0:4] = r1_ref[0:4]
    g_ref[4:8] = r2_ref[0:4]
    g_ref[20:24] = r3_ref[0:4]
    for q in range(4):
        a = c1_ref[q]
        g_ref[8 + q] = jnp.where(a >= 0, r1_ref[jnp.maximum(a, 0)], 0.0)
        b = c2_ref[q]
        c = c1_ref[jnp.maximum(b, 0)]
        g_ref[12 + q] = jnp.where((b >= 0) & (c >= 0), r1_ref[jnp.maximum(c, 0)], 0.0)
        g_ref[16 + q] = jnp.where(b >= 0, r2_ref[jnp.maximum(b, 0)], 0.0)


def panels(c1, c2, k):
    smem = pl.BlockSpec(memory_space=pltpu.SMEM)
    vmem = pl.BlockSpec(memory_space=pltpu.VMEM)
    return pl.pallas_call(
        panel_kernel,
        out_shape=[jax.ShapeDtypeStruct((BLOCKS, 4, 128), F32)] * 3
        + [
            jax.ShapeDtypeStruct((24, 4, 128), F32),
            jax.ShapeDtypeStruct((COLS, 3, TC, 4, 128), F32),
        ],
        in_specs=[smem, smem, vmem],
        out_specs=[vmem] * 5,
        scratch_shapes=[pltpu.VMEM((BLOCKS, 8, 128), F32)],
        compiler_params=pltpu.CompilerParams(vmem_limit_bytes=32 << 20),
    )(c1, c2, k)


def extend_kernel(c1_ref, c2_ref, m1_ref, m2_ref, a_ref, o_ref, s_ref):
    def moved(src, m_ref, c):
        cc = jnp.maximum(c, 0)
        t = cc // ROWS
        i = cc % ROWS
        x = [src[i, j, t] for j in range(COLS)]
        x = x + [pltpu.roll(x[j], 7, 0) for j in range(MAXD)]
        out = []
        for j in range(COLS):
            acc = m_ref[0, j] * x[j]
            for d in range(1, MAXD + 1):
                acc = acc + m_ref[d, j] * x[j + d]
            out.append(jnp.where(c >= 0, acc, 0.0))
        return out

    def first(p, carry):
        got = moved(a_ref, m1_ref, c1_ref[p])
        t = p // ROWS
        i = p % ROWS
        for j in range(COLS):
            s_ref[i, j, t] = a_ref[i, j, TR + t] + got[j]
        return carry

    lax.fori_loop(0, BLOCKS, first, 0)

    def second(p, carry):
        got = moved(s_ref, m2_ref, c2_ref[p])
        t = p // ROWS
        i = p % ROWS
        for j in range(COLS):
            o_ref[i, j, t] = got[j]
        return carry

    lax.fori_loop(0, BLOCKS, second, 0)


def extended(c1, c2, m1, m2, a):
    smem = pl.BlockSpec(memory_space=pltpu.SMEM)
    vmem = pl.BlockSpec(memory_space=pltpu.VMEM)
    shape = (ROWS, COLS, TR, TC, 128)
    return pl.pallas_call(
        extend_kernel,
        out_shape=jax.ShapeDtypeStruct(shape, F32),
        in_specs=[smem, smem, vmem, vmem, vmem],
        out_specs=vmem,
        scratch_shapes=[pltpu.VMEM(shape, F32)],
        compiler_params=pltpu.CompilerParams(vmem_limit_bytes=32 << 20),
    )(c1, c2, m1, m2, a)


def dot(a, b):
    return jnp.dot(a, b, precision=HI, preferred_element_type=F32)


def dot_t(a, b):
    return lax.dot_general(
        a, b, (((1,), (1,)), ((), ())), precision=HI, preferred_element_type=F32
    )


def child_of(block_map):
    blocks = jnp.arange(BLOCKS, dtype=jnp.int32)
    hit = block_map[None, :] == blocks[:, None]
    ids = jnp.arange(block_map.shape[0], dtype=jnp.int32) + (PIVOTS // TILE + 1)
    return jnp.sum(jnp.where(hit, ids[None, :], 0), axis=1) - 1


def column_masks(child):
    blocks = jnp.arange(BLOCKS, dtype=jnp.int32)
    hits = jnp.stack([child == blocks + d for d in range(MAXD + 1)])
    hits = hits.reshape(MAXD + 1, TC, COLS).transpose(0, 2, 1).astype(F32)
    return jnp.broadcast_to(hits[..., None], (MAXD + 1, COLS, TC, 128))


def one_hot(child):
    return (child[:, None] == jnp.arange(BLOCKS, dtype=jnp.int32)[None, :]).astype(F32)


def to_all(rows):
    n = rows.shape[0]
    many = jnp.broadcast_to(rows[None], (128, n, PIVOTS))
    return lax.all_to_all(many, BOTH, 0, 0, tiled=True).transpose(1, 0, 2)


def after(x, y):
    return lax.optimization_barrier((x, y))


def per_device(front_first, front_second, front_third, map_second, map_third):
    first = front_first.reshape(TR, TILE, TC, TILE)
    second = front_second.reshape(TR, TILE, TC, TILE)
    third = front_third.reshape(TR, TILE, TC, TILE)
    c1 = child_of(map_second)
    c2 = child_of(map_third)
    e1 = one_hot(c1)
    e2 = one_hot(c2)

    packed = jnp.concatenate([first[:, :, 0:2], second[:, :, 0:1], third[:, :, 0:1]], axis=2)
    packed = packed.transpose(1, 0, 2, 3).reshape(128, 16, 128)
    packed = lax.all_to_all(packed, BOTH, 0, 0, tiled=True).reshape(ROWS, COLS, 16, 128)
    r1, r2, r3, g, h = panels(c1, c2, packed)
    r1, r2, r3 = (r.reshape(BLOCKS, PIVOTS) for r in (r1, r2, r3))
    g = g.reshape(24, PIVOTS)

    g3 = lax.all_gather(g[12:24], BOTH, axis=1).reshape(3, PIVOTS, PIVOTS)
    d1 = to_all(g[0:4]).reshape(PIVOTS, PIVOTS)
    g_next, d1 = after(g[4:12], d1)
    g2 = to_all(g_next).reshape(2, PIVOTS, PIVOTS)
    w1 = inverse_factor(d1)

    (h, w1), g2 = after((h, w1), g2)
    cols = lax.all_to_all(h.reshape(COLS, 3, TC, PIVOTS), "col", 0, 0, tiled=True)
    cols = lax.all_gather(cols.transpose(1, 2, 0, 3), "row", axis=0)

    lp1 = dot_t(g2[1], w1)
    d2 = g2[0] - dot_t(lp1, lp1)
    (first, second), d2 = after((first, second), d2)
    moving = jnp.concatenate([first.transpose(1, 0, 2, 3), second.transpose(1, 0, 2, 3)], axis=1)
    moving = lax.all_to_all(moving, BOTH, 0, 0, tiled=True)
    w2 = inverse_factor(d2)

    lp1x = dot_t(g3[0], w1)
    lp2 = dot_t(g3[1] - dot_t(lp1x, lp1), w2)
    w3 = inverse_factor(g3[2] - dot_t(lp1x, lp1x) - dot_t(lp2, lp2))

    l1 = dot_t(r1, w1)
    l1x = dot(e1, l1)
    l1xx = dot(e2, l1x)
    l2 = dot_t(r2 - dot_t(l1x, lp1), w2)
    l2x = dot(e2, l2)
    l3 = dot_t(r3 - dot_t(l1xx, lp1x) - dot_t(l2x, lp2), w3)
    rows = jnp.stack([l1, l2, l1xx, l2x, l3]).reshape(5, TR, ROWS, PIVOTS)
    rows, moving = after(rows, moving)
    rows = lax.all_to_all(rows.transpose(2, 0, 1, 3), "row", 0, 0, tiled=True)
    rows = lax.all_gather(rows.transpose(1, 2, 0, 3), "col", axis=0)
    rows = rows.transpose(1, 2, 3, 0, 4).reshape(5, TR * TILE, PIVOTS)

    back = extended(
        c1,
        c2,
        column_masks(c1),
        column_masks(c2),
        moving.reshape(ROWS, COLS, 2 * TR, TC, TILE),
    )
    back = lax.all_to_all(back.reshape(128, TR, TC, TILE), BOTH, 0, 0, tiled=True)
    assembled = third + back.transpose(1, 0, 2, 3)

    cols = cols.transpose(1, 2, 0, 3, 4).reshape(3, TC * TILE, PIVOTS)
    l1c = dot_t(cols[0], w1)
    l2c = dot_t(cols[1] - dot_t(l1c, lp1), w2)
    l3c = dot_t(cols[2] - dot_t(l1c, lp1x) - dot_t(l2c, lp2), w3)
    lower_first = rows[0]
    lower_second = rows[1]
    l3r = rows[4]
    update = dot_t(rows[2], l1c) + dot_t(rows[3], l2c) + dot_t(l3r, l3c)
    schur = assembled - update.reshape(TR, TILE, TC, TILE)
    pivot_blocks = PIVOTS // TILE
    row_keep = jnp.arange(TR) * ROWS + lax.axis_index("row") >= pivot_blocks
    col_keep = jnp.arange(TC) * COLS + lax.axis_index("col") >= pivot_blocks
    keep = row_keep[:, None, None, None] & col_keep[None, None, :, None]
    schur = jnp.where(keep, schur, 0.0)
    out = (1, TR, TILE, PIVOTS)
    return (
        lower_first.reshape(out),
        lower_second.reshape(out),
        l3r.reshape(out),
        schur.reshape(1, TR, TILE, 1, TC, TILE),
    )


def solution(mesh):
    front = P("row", None, None, "col", None, None)
    lower = P("row", None, None, None)
    return jax.shard_map(
        per_device,
        mesh=mesh,
        in_specs=(front, front, front, P(), P()),
        out_specs=(lower, lower, lower, front),
        check_vma=False,
    )
```

profile of v0, /device:TPU:1, one launch (start us, length us, event | category | flops | bytes accessed | tf_op | source)
XLA Modules:
  0.0 343.4 jit_solution(16119611677179097636)
XLA Ops:
  14.0 11.5 %all-to-all-start = ((f32[128,16,128]{2,1,0:T(8,128)}), f32[128,16,128]{2,1,0:T(8,128)S(1)}, u32[]{:S(2)}, u32[]{:S(2)}) async-start(f32[128,16,128]{2,1,0:T(8,128)} %copy.160), calls=%async_computation | async-start | bytes 2097152 | tf_op jit(solution)/shard_map/all_to_all | solution.py:322
  25.7 19.0 %all-to-all-done = f32[128,16,128]{2,1,0:T(8,128)S(1)} async-done(((f32[128,16,128]{2,1,0:T(8,128)}), f32[128,16,128]{2,1,0:T(8,128)S(1)}, u32[]{:S(2)}, u32[]{:S(2)}) %all-to-all-start) | async-done | bytes 1048608 | tf_op jit(solution)/shard_map/all_to_all | solution.py:322
  44.7 6.4 %shard_map.84 = (f32[64,4,128]{2,1,0:T(4,128)S(1)}, f32[64,4,128]{2,1,0:T(4,128)S(1)}, f32[64,4,128]{2,1,0:T(4,128)S(1)}, f32[24,4,128]{2,1,0:T(4,128)S(1)}, f32[8,3,8,4,128]{4,3,2,1,0:T(4,128)S(1)}) custom-call(s32[64]{0:T(128)S(1)} %get-tuple-element.78.c1_ref, s32[64]{0:T(128)S(1)} %get-tuple-element.77.c2_ref, f32[16,8,16,128]{3,2,1,0:T(8,128)S(1)} %bitcast.145), custom_call_target="tpu_custom_call" | custom-call | tf_op jit(solution)/shard_map/pallas_call | solution.py:209
  52.9 4.6 %all-to-all-start.1 = ((f32[128,4,512]{2,1,0:T(4,128)}), f32[128,4,512]{2,1,0:T(4,128)S(1)}, u32[]{:S(2)}, u32[]{:S(2)}) async-start(f32[128,4,512]{2,1,0:T(4,128)} %broadcast_in_dim.39), calls=%async_computation.1 | async-start | bytes 2097152 | tf_op jit(solution)/shard_map/all_to_all | solution.py:304
  57.5 19.5 %all-to-all-done.1 = f32[128,4,512]{2,1,0:T(4,128)S(1)} async-done(((f32[128,4,512]{2,1,0:T(4,128)}), f32[128,4,512]{2,1,0:T(4,128)S(1)}, u32[]{:S(2)}, u32[]{:S(2)}) %all-to-all-start.1) | async-done | bytes 1048608 | tf_op jit(solution)/shard_map/all_to_all | solution.py:304
  79.0 5.7 %all-to-all-start.2 = ((f32[128,8,512]{2,1,0:T(8,128)}), f32[128,8,512]{2,1,0:T(8,128)}, u32[]{:S(2)}, u32[]{:S(2)}) async-start(f32[128,8,512]{2,1,0:T(8,128)} %broadcast_in_dim.72), calls=%async_computation.2 | async-start | bytes 4194304 | tf_op jit(solution)/shard_map/all_to_all | solution.py:304
  85.3 22.2 %shard_map.85 = f32[512,512]{1,0:T(8,128)S(1)} custom-call(f32[512,512]{1,0:T(8,128)S(1)} %bitcast.146), custom_call_target="tpu_custom_call" | custom-call | flops 24999999488 | bytes 2000000 | tf_op jit(solution)/shard_map/pallas_call | solution.py:135
  107.5 8.9 %all-to-all-done.2 = f32[128,8,512]{2,1,0:T(8,128)} async-done(((f32[128,8,512]{2,1,0:T(8,128)}), f32[128,8,512]{2,1,0:T(8,128)}, u32[]{:S(2)}, u32[]{:S(2)}) %all-to-all-start.2) | async-done | bytes 2097184 | tf_op jit(solution)/shard_map/all_to_all | solution.py:304
  116.3 4.1 %copy.162 = f32[8,128,512]{2,1,0:T(8,128)} copy(f32[8,128,512]{2,0,1:T(8,128)} %bitcast.8) | data formatting | bytes 4194304 | tf_op jit(solution)/shard_map/transpose | solution.py:304
  120.6 14.0 %all_to_all.35 = f32[8,3,8,512]{3,2,1,0:T(8,128)S(1)} all-to-all(f32[8,3,8,512]{3,2,1,0:T(8,128)S(1)} %reshape.321), channel_id=1, replica_groups=mesh['row'=16,'col'=8] {'col'}, dimensions={0} | all-to-all | bytes 786432 | tf_op jit(solution)/shard_map/all_to_all | solution.py:334
  142.8 4.4 %copy.171 = f32[128,8,8,128]{3,2,1,0:T(8,128)} copy(f32[128,8,8,128]{3,0,2,1:T(8,128)S(1)} %pad_maximum_fusion) | data formatting | bytes 8388608 | tf_op jit(solution)/shard_map/concatenate | solution.py:340
  147.2 5.6 %all-to-all-start.3 = ((f32[128,8,8,128]{3,2,1,0:T(8,128)}), f32[128,8,8,128]{3,2,1,0:T(8,128)}, u32[]{:S(2)}, u32[]{:S(2)}) async-start(f32[128,8,8,128]{3,2,1,0:T(8,128)} %copy.171), calls=%async_computation.3 | async-start | bytes 8388608 | tf_op jit(solution)/shard_map/all_to_all | solution.py:341
  156.3 22.6 %shard_map.86 = f32[512,512]{1,0:T(8,128)S(1)} custom-call(f32[512,512]{1,0:T(8,128)S(1)} %convolution_subtract_fusion.3.d_ref), custom_call_target="tpu_custom_call" | custom-call | flops 24999999488 | bytes 2000000 | tf_op jit(solution)/shard_map/pallas_call | solution.py:135
  199.3 22.2 %shard_map.87 = f32[512,512]{1,0:T(8,128)S(1)} custom-call(f32[512,512]{1,0:T(8,128)S(1)} %convolution_subtract_fusion.d_ref), custom_call_target="tpu_custom_call" | custom-call | flops 24999999488 | bytes 2000000 | tf_op jit(solution)/shard_map/pallas_call | solution.py:135
  223.4 24.1 %all_to_all.36 = f32[16,5,4,512]{3,2,1,0:T(4,128)S(1)} all-to-all(f32[16,5,4,512]{3,2,1,0:T(4,128)} %bitcast.22), channel_id=1, replica_groups=mesh['row'=16,'col'=8] {'row'}, dimensions={0} | all-to-all | bytes 1310720 | tf_op jit(solution)/shard_map/all_to_all | solution.py:356
  249.3 5.7 %shard_map.88 = f32[16,8,4,8,128]{4,3,2,1,0:T(8,128)S(1)} custom-call(s32[64]{0:T(128)S(1)} %get-tuple-element.78.c1_ref, s32[64]{0:T(128)S(1)} %get-tuple-element.77.c2_ref, f32[5,8,8,128]{3,2,1,0:T(8,128)S(1)} %broadcast_in_dim.74.m1_ref, f32[5,8,8,128]{3,2,1,0:T(8,128)S(1)} %broadcast_in_dim.75.m2_ref, f32[16,8,8,8,128]{4,3,2,1,0:T(8,128)} %bitcast.32.a_ref), custom_call_target="tpu_custom_call" | custom-call | tf_op jit(solution)/shard_map/pallas_call | solution.py:263
  256.3 7.0 %all-to-all-start.5 = ((f32[128,4,8,128]{3,2,1,0:T(8,128)}), f32[128,4,8,128]{3,2,1,0:T(8,128)}, u32[]{:S(2)}, u32[]{:S(2)}) async-start(f32[128,4,8,128]{3,2,1,0:T(8,128)} %bitcast.144), calls=%async_computation.5 | async-start | bytes 4194304 | tf_op jit(solution)/shard_map/all_to_all | solution.py:367
  263.4 3.7 %fusion.30 = (f32[1,8,16,8,512]{4,3,1,0,2:T(8,128)S(1)}, f32[1,8,16,8,512]{4,3,1,0,2:T(8,128)S(1)}, f32[1,8,16,8,512]{4,3,1,0,2:T(8,128)S(1)}) fusion(f32[3,8,16,8,512]{4,3,1,0,2:T(8,128)} %bitcast.156), kind=kLoop, calls=%fused_computation.83 | loop fusion | bytes 12582912 | tf_op jit(solution)/shard_map/slice | solution.py:373
  274.8 3.9 %bitcast_subtract_fusion.1 = f32[1024,512]{1,0:T(8,128)S(1)} fusion(f32[1,8,16,8,512]{4,3,2,1,0:T(8,128)S(1)} %copy.183, f32[1024,512]{1,0:T(8,128)S(1)} %fusion.38, f32[512,512]{1,0:T(8,128)S(1)} %copy-done.3), kind=kOutput, calls=%fused_computation.3 | convolution fusion | flops 3221749760 | bytes 7340032 | tf_op jit(solution)/shard_map/dot_general | solution.py:278
  286.0 4.8 %fusion.43 = f32[1024,512]{1,0:T(8,128)} fusion(f32[1024,512]{1,0:T(8,128)S(1)} %fusion, f32[512,512]{1,0:T(8,128)S(1)} %shard_map.87), kind=kOutput, calls=%fused_computation.96 | convolution fusion | flops 3221225472 | bytes 5242880 | tf_op jit(solution)/shard_map/dot_general | solution.py:278
  290.8 15.6 %all-gather.8.cloned.1.call-done = f32[40,4,16,512]{3,2,1,0:T(8,128)} async-done(((f32[5,4,16,512]{3,2,1,0:T(8,128)}), f32[40,4,16,512]{3,2,1,0:T(8,128)}) %all-gather.8.cloned.1.call-update) | async-done | bytes 5242896 | tf_op jit(solution)/shard_map/all_gather | solution.py:357
  306.5 4.7 %fusion.31 = (f32[1,4,16,8,512]{4,2,1,0,3:T(8,128)S(1)}, f32[1,4,16,8,512]{4,2,1,0,3:T(8,128)S(1)}, f32[1,4,16,8,512]{4,2,1,0,3:T(8,128)S(1)}, f32[1,4,16,8,512]{4,2,1,0,3:T(8,128)}, f32[1,4,16,8,512]{4,2,1,0,3:T(8,128)}) fusion(f32[5,4,16,8,512]{4,2,1,0,3:T(8,128)} %bitcast.157), kind=kLoop, calls=%fused_computation.84 | loop fusion | bytes 10485760 | tf_op jit(solution)/shard_map/slice | solution.py:377
  320.8 4.0 %add_bitcast_fusion = f32[64,8,8,128]{3,1,2,0:T(8,128)S(1)} fusion(f32[512,1024]{1,0:T(8,128)S(1)} %fusion.39, f32[512,1024]{1,0:T(8,128)S(1)} %fusion.41, f32[512,512]{1,0:T(8,128)S(1)} %bitcast.158, f32[1024,512]{1,0:T(8,128)S(1)} %copy-done.18), kind=kOutput, calls=%fused_computation.11 | convolution fusion | flops 3222274048 | bytes 9437184 | tf_op jit(solution)/shard_map/dot_general | solution.py:278
  326.7 4.2 %fusion.3 = f32[1,4,128,1,8,128]{5,2,4,1,3,0:T(8,128)S(1)} fusion(f32[4,128,8,128]{3,2,1,0:T(8,128)} %bitcast.155, f32[128,4,8,128]{3,2,1,0:T(8,128)} %all-to-all-done.5, pred[4,8]{1,0:T(4,128)(4,1)S(1)} %broadcast_and_fusion, f32[1,4,128,1,8,128]{5,4,3,2,1,0:T(8,128)S(1)} %copy-done.17), kind=kLoop, calls=%fused_computation.7 | loop fusion | flops 1572864 | bytes 8388640 | tf_op jit(solution)/shard_map/reshape | solution.py:389
  (147 shorter events, 80.3 us)
Async XLA Ops:
  7.2 3.2 copy-start.16
  12.4 13.2 %copy-start.24 = (s32[60]{0:T(128)S(1)}, s32[60]{0:T(128)}, u32[]{:S(2)}) copy-start(s32[60]{0:T(128)} %param.9) | copy-start | bytes 724
  12.4 13.2 %copy-start.25 = (s32[60]{0:T(128)S(1)}, s32[60]{0:T(128)}, u32[]{:S(2)}) copy-start(s32[60]{0:T(128)} %param.8) | copy-start | bytes 724
  14.0 30.7 %all-to-all-start = ((f32[128,16,128]{2,1,0:T(8,128)}), f32[128,16,128]{2,1,0:T(8,128)S(1)}, u32[]{:S(2)}, u32[]{:S(2)}) async-start(f32[128,16,128]{2,1,0:T(8,128)} %copy.160), calls=%async_computation | async-start | bytes 2097152 | tf_op jit(solution)/shard_map/all_to_all | solution.py:322
  25.5 157.3 %all-gather.6.cloned.1.call-start = ((), (), s32[]{:S(2)}) async-start(), calls=%async_computation.7 | async-start | bytes 4227072 | tf_op jit(solution)/shard_map/all_gather | solution.py:327
  52.9 24.2 %all-to-all-start.1 = ((f32[128,4,512]{2,1,0:T(4,128)}), f32[128,4,512]{2,1,0:T(4,128)S(1)}, u32[]{:S(2)}, u32[]{:S(2)}) async-start(f32[128,4,512]{2,1,0:T(4,128)} %broadcast_in_dim.39), calls=%async_computation.1 | async-start | bytes 2097152 | tf_op jit(solution)/shard_map/all_to_all | solution.py:304
  79.0 37.3 %all-to-all-start.2 = ((f32[128,8,512]{2,1,0:T(8,128)}), f32[128,8,512]{2,1,0:T(8,128)}, u32[]{:S(2)}, u32[]{:S(2)}) async-start(f32[128,8,512]{2,1,0:T(8,128)} %broadcast_in_dim.72), calls=%async_computation.2 | async-start | bytes 4194304 | tf_op jit(solution)/shard_map/all_to_all | solution.py:304
  84.7 178.7 %all-gather.10.cloned.1.call-start = ((), (), s32[]{:S(2)}) async-start(), calls=%async_computation.9 | async-start | bytes 6684672 | tf_op jit(solution)/shard_map/all_gather | solution.py:335
  138.8 16.4 %copy-start.1 = (f32[512,512]{1,0:T(8,128)}, f32[512,512]{1,0:T(8,128)S(1)}, u32[]{:S(2)}) copy-start(f32[512,512]{1,0:T(8,128)S(1)} %fusion.4) | copy-start | bytes 3145732
  138.8 3.5 %copy-start.13 = (f32[4,128,8,128]{3,1,2,0:T(8,128)S(1)}, f32[4,128,8,128]{3,1,2,0:T(8,128)}, u32[]{:S(2)}) copy-start(f32[4,128,8,128]{3,1,2,0:T(8,128)} %copy-done.12) | copy-start | bytes 6291460
  138.8 3.5 %copy-start.15 = (f32[4,128,8,128]{3,1,2,0:T(8,128)S(1)}, f32[4,128,8,128]{3,1,2,0:T(8,128)}, u32[]{:S(2)}) copy-start(f32[4,128,8,128]{3,1,2,0:T(8,128)} %copy-done.14) | copy-start | bytes 6291460
  147.2 76.1 %all-to-all-start.3 = ((f32[128,8,8,128]{3,2,1,0:T(8,128)}), f32[128,8,8,128]{3,2,1,0:T(8,128)}, u32[]{:S(2)}, u32[]{:S(2)}) async-start(f32[128,8,8,128]{3,2,1,0:T(8,128)} %copy.171), calls=%async_computation.3 | async-start | bytes 8388608 | tf_op jit(solution)/shard_map/all_to_all | solution.py:341
  152.8 153.6 %all-gather.8.cloned.1.call-start = ((), (), s32[]{:S(2)}) async-start(), calls=%async_computation.8 | async-start | bytes 5898240 | tf_op jit(solution)/shard_map/all_gather | solution.py:357
  189.0 6.4 %copy-start.4 = (f32[512,512]{1,0:T(8,128)}, f32[512,512]{1,0:T(8,128)S(1)}, u32[]{:S(2)}) copy-start(f32[512,512]{1,0:T(8,128)S(1)} %fusion.35) | copy-start | bytes 3145732
  194.3 3.2 copy-start.8
  256.3 70.3 %all-to-all-start.5 = ((f32[128,4,8,128]{3,2,1,0:T(8,128)}), f32[128,4,8,128]{3,2,1,0:T(8,128)}, u32[]{:S(2)}, u32[]{:S(2)}) async-start(f32[128,4,8,128]{3,2,1,0:T(8,128)} %bitcast.144), calls=%async_computation.5 | async-start | bytes 4194304 | tf_op jit(solution)/shard_map/all_to_all | solution.py:367
  267.8 3.5 %copy-start.5 = (f32[512,512]{1,0:T(8,128)S(1)}, f32[512,512]{1,0:T(8,128)}, u32[]{:S(2)}) copy-start(f32[512,512]{1,0:T(8,128)} %copy-done.4) | copy-start | bytes 3145732
  271.3 3.5 %copy-start.6 = (f32[1024,512]{1,0:T(8,128)}, f32[1024,512]{1,0:T(8,128)S(1)}, u32[]{:S(2)}) copy-start(f32[1024,512]{1,0:T(8,128)S(1)} %fusion.38) | copy-start | bytes 6291460
  271.3 3.5 %copy-start.3 = (f32[512,512]{1,0:T(8,128)S(1)}, f32[512,512]{1,0:T(8,128)}, u32[]{:S(2)}) copy-start(f32[512,512]{1,0:T(8,128)} %copy-done.1) | copy-start | bytes 3145732
  278.8 3.5 %copy-start.9 = (f32[512,512]{1,0:T(8,128)S(1)}, f32[512,512]{1,0:T(8,128)}, u32[]{:S(2)}) copy-start(f32[512,512]{1,0:T(8,128)} %copy-done.8) | copy-start | bytes 3145732
  282.3 3.7 %copy-start.10 = (f32[1024,512]{1,0:T(8,128)}, f32[1024,512]{1,0:T(8,128)S(1)}, u32[]{:S(2)}) copy-start(f32[1024,512]{1,0:T(8,128)S(1)} %fusion.40) | copy-start | bytes 6291460
  313.2 7.6 %copy-start.19 = (f32[1,4,16,8,512]{4,3,2,1,0:T(8,128)}, f32[1,4,16,8,512]{4,3,2,1,0:T(8,128)S(1)}, u32[]{:S(2)}) copy-start(f32[1,4,16,8,512]{4,3,2,1,0:T(8,128)S(1)} %copy.225) | copy-start | bytes 3145732
  313.5 3.6 %copy-start.7 = (f32[1024,512]{1,0:T(8,128)S(1)}, f32[1024,512]{1,0:T(8,128)}, u32[]{:S(2)}) copy-start(f32[1024,512]{1,0:T(8,128)} %copy-done.6) | copy-start | bytes 6291460
  317.1 3.6 %copy-start.18 = (f32[1024,512]{1,0:T(8,128)S(1)}, f32[1024,512]{1,0:T(8,128)}, u32[]{:S(2)}) copy-start(f32[1024,512]{1,0:T(8,128)} %fusion.43) | copy-start | bytes 6291460
  (10 other events, 17.8 us)
Sparse Core Ops, SparseCore 0:
  51.9 87.7 all-gather.5
  141.8 103.5 all-gather.9
  248.6 57.7 all-gather.7
where the time goes:
time: 348 us; the launch traced here: 343 us
  Pallas kernels  79 us (23%)
  waiting for transfers between devices  63.1 us (18%)
  matrix products  57.6 us (17%)
  local copies, waits for them, and re-layouts  50.4 us (14%)
  blocking collectives  38.1 us (11%)
  starting transfers between devices  35.3 us (10%)
  between operations  14.8 us (4%)
  other arithmetic  5.18 us (1%)
    pallas_call x3, Pallas kernels, inverse_factor(): pl.pallas_call(chol_kernel, out_shape=jax.ShapeDtypeStruct((PIVOTS, PIVOT...  66.9 us
    dot_general x22, matrix products, dot_t(): lax.dot_general(a, b, (((1,), (1,)), ((), ())), precision=HI, preferred_e...  56.9 us
    all_to_all x2, waiting for transfers between devices, to_all(): return lax.all_to_all(many, BOTH, 0, 0, tiled=True).transpose(1, 0, 2)  28.4 us
    all_to_all x1, blocking collectives, per_device(): rows = lax.all_to_all(rows.transpose(2, 0, 1, 3), 'row', 0, 0, tiled=True)  24.1 us
    all_to_all x1, waiting for transfers between devices, per_device(): lax.all_to_all(packed, BOTH, 0, 0, tiled=True).reshape(ROWS, COLS, 16, 128)  19 us
    all_gather x1, waiting for transfers between devices, per_device(): rows = lax.all_gather(rows.transpose(1, 2, 0, 3), 'col', axis=0)  15.6 us
    all_to_all x1, blocking collectives, per_device(): lax.all_to_all(h.reshape(COLS, 3, TC, PIVOTS), 'col', 0, 0, tiled=True)  14 us
    unnamed x65, local copies, waits for them, and re-layouts  11.8 us
  transfers between devices with their start and end apart: 8, of which 4 were waited for; matrix products, arithmetic and copies ran while one was open for 27% of the time, Pallas kernels for 21%

commit v1 on v0

--- a/solution.py
+++ b/solution.py
@@ -143,15 +143,26 @@
     )(d)
 
 
-def panel_kernel(c1_ref, c2_ref, k_ref, r1_ref, r2_ref, r3_ref, g_ref, h_ref, s_ref):
+SMEM = pl.BlockSpec(memory_space=pltpu.SMEM)
+VMEM = pl.BlockSpec(memory_space=pltpu.VMEM)
+
+
+def assemble(c1_ref, c2_ref, k_ref, r1_ref, r2_ref, r3_ref, s_ref, n1, n2, n3):
     def row(i, j, t, c):
         return k_ref[i, j, pl.ds(t * 4 + c, 1), :]
 
-    def first(p, carry):
+    def load(p, carry):
         t = p // ROWS
         i = p % ROWS
         for q in range(4):
             r1_ref[p, q : q + 1, :] = row(i, q, t, 0)
+        return carry
+
+    lax.fori_loop(0, n1, load, 0)
+
+    def first(p, carry):
+        t = p // ROWS
+        i = p % ROWS
         cp = c1_ref[p]
         cc = jnp.maximum(cp, 0)
         tt = cc // ROWS
@@ -167,7 +178,7 @@
                 r2_ref[p, q : q + 1, :] = val
         return carry
 
-    lax.fori_loop(0, BLOCKS, first, 0)
+    lax.fori_loop(0, n2, first, 0)
 
     def second(p, carry):
         t = p // ROWS
@@ -180,6 +191,19 @@
             got = s_ref[cc, pl.ds(qq, 1), :]
             got = jnp.where((cp >= 0) & (cq >= 0), got, 0.0)
             r3_ref[p, q : q + 1, :] = row(i, q, t, 3) + got
+        return carry
+
+    lax.fori_loop(0, n3, second, 0)
+
+
+def panel_kernel(c1_ref, c2_ref, k_ref, r1_ref, r2_ref, r3_ref, h_ref, s_ref):
+    assemble(
+        c1_ref, c2_ref, k_ref, r1_ref, r2_ref, r3_ref, s_ref, BLOCKS, BLOCKS, BLOCKS
+    )
+
+    def column_side(p, carry):
+        cp = c2_ref[p]
+        cc = jnp.maximum(cp, 0)
         c12 = c1_ref[cc]
         j = p % COLS
         s = p // COLS
@@ -190,7 +214,11 @@
         h_ref[j, 2, s] = r3_ref[p]
         return carry
 
-    lax.fori_loop(0, BLOCKS, second, 0)
+    lax.fori_loop(0, BLOCKS, column_side, 0)
+
+
+def pivot_kernel(c1_ref, c2_ref, k_ref, g_ref, r1_ref, r2_ref, r3_ref, s_ref):
+    assemble(c1_ref, c2_ref, k_ref, r1_ref, r2_ref, r3_ref, s_ref, 12, 8, 4)
     g_ref[0:4] = r1_ref[0:4]
     g_ref[4:8] = r2_ref[0:4]
     g_ref[20:24] = r3_ref[0:4]
@@ -204,20 +232,45 @@
 
 
 def panels(c1, c2, k):
-    smem = pl.BlockSpec(memory_space=pltpu.SMEM)
-    vmem = pl.BlockSpec(memory_space=pltpu.VMEM)
     return pl.pallas_call(
         panel_kernel,
         out_shape=[jax.ShapeDtypeStruct((BLOCKS, 4, 128), F32)] * 3
-        + [
-            jax.ShapeDtypeStruct((24, 4, 128), F32),
-            jax.ShapeDtypeStruct((COLS, 3, TC, 4, 128), F32),
-        ],
-        in_specs=[smem, smem, vmem],
-        out_specs=[vmem] * 5,
+        + [jax.ShapeDtypeStruct((COLS, 3, TC, 4, 128), F32)],
+        in_specs=[SMEM, SMEM, VMEM],
+        out_specs=[VMEM] * 4,
         scratch_shapes=[pltpu.VMEM((BLOCKS, 8, 128), F32)],
         compiler_params=pltpu.CompilerParams(vmem_limit_bytes=32 << 20),
     )(c1, c2, k)
+
+
+def pivots(c1, c2, k):
+    return pl.pallas_call(
+        pivot_kernel,
+        out_shape=jax.ShapeDtypeStruct((24, 4, 128), F32),
+        in_specs=[SMEM, SMEM, VMEM],
+        out_specs=VMEM,
+        scratch_shapes=[pltpu.VMEM((12, 4, 128), F32)]
+        + [pltpu.VMEM((8, 4, 128), F32)] * 2
+        + [pltpu.VMEM((8, 8, 128), F32)],
+        compiler_params=pltpu.CompilerParams(vmem_limit_bytes=32 << 20),
+    )(c1, c2, k)
+
+
+def pack_kernel(a_ref, b_ref, o_ref):
+    o_ref[:, 0, 0] = a_ref[0]
+    o_ref[:, 1, 0] = b_ref[0]
+
+
+def pack(a, b):
+    block = pl.BlockSpec((1, TILE, TC, TILE), lambda t: (t, 0, 0, 0))
+    return pl.pallas_call(
+        pack_kernel,
+        grid=(TR,),
+        out_shape=jax.ShapeDtypeStruct((TILE, 2, TR, TC, TILE), F32),
+        in_specs=[block, block],
+        out_specs=pl.BlockSpec((TILE, 2, 1, TC, TILE), lambda t: (0, 0, t, 0, 0)),
+        compiler_params=pltpu.CompilerParams(vmem_limit_bytes=32 << 20),
+    )(a, b)
 
 
 def extend_kernel(c1_ref, c2_ref, m1_ref, m2_ref, a_ref, o_ref, s_ref):
@@ -274,9 +327,9 @@
     return jnp.dot(a, b, precision=HI, preferred_element_type=F32)
 
 
-def dot_t(a, b):
+def dot_t(a, b, precision=HI):
     return lax.dot_general(
-        a, b, (((1,), (1,)), ((), ())), precision=HI, preferred_element_type=F32
+        a, b, (((1,), (1,)), ((), ())), precision=precision, preferred_element_type=F32
     )
 
 
@@ -298,10 +351,19 @@
     return (child[:, None] == jnp.arange(BLOCKS, dtype=jnp.int32)[None, :]).astype(F32)
 
 
-def to_all(rows):
+def own_rows(rows, later):
     n = rows.shape[0]
-    many = jnp.broadcast_to(rows[None], (128, n, PIVOTS))
-    return lax.all_to_all(many, BOTH, 0, 0, tiled=True).transpose(1, 0, 2)
+    half = PIVOTS // 2
+    many = rows.reshape(n, TR, ROWS, 2, half).transpose(2, 3, 0, 1, 4)
+    many = jnp.broadcast_to(many[:, None], (ROWS, COLS // 2, 2, n, TR, half))
+    mine = lax.all_to_all(
+        many.reshape(ROWS * COLS, n, TR, half), BOTH, 0, 0, tiled=True
+    )
+    mine, later = after(mine, later)
+    other = lax.ppermute(mine, "col", [(j, j ^ 1) for j in range(COLS)])
+    even = lax.axis_index("col") % 2 == 0
+    halves = [jnp.where(even, mine, other), jnp.where(even, other, mine)]
+    return jnp.concatenate(halves, axis=3).transpose(1, 2, 0, 3), later
 
 
 def after(x, y):
@@ -318,32 +380,43 @@
     e2 = one_hot(c2)
 
     packed = jnp.concatenate([first[:, :, 0:2], second[:, :, 0:1], third[:, :, 0:1]], axis=2)
-    packed = packed.transpose(1, 0, 2, 3).reshape(128, 16, 128)
-    packed = lax.all_to_all(packed, BOTH, 0, 0, tiled=True).reshape(ROWS, COLS, 16, 128)
-    r1, r2, r3, g, h = panels(c1, c2, packed)
+    packed = packed.transpose(1, 0, 2, 3)
+
+    top = lax.all_to_all(packed[:, 0], BOTH, 0, 0, tiled=True)
+    g = pivots(c1, c2, top.reshape(ROWS, COLS, 4, 128)).reshape(24, PIVOTS)
+    packed, g = after(packed, g)
+    pivot = lax.all_gather(g, BOTH, axis=1).reshape(6, PIVOTS, PIVOTS)
+
+    packed = lax.all_to_all(packed.reshape(128, 16, 128), BOTH, 0, 0, tiled=True)
+    r1, r2, r3, h = panels(c1, c2, packed.reshape(ROWS, COLS, 16, 128))
     r1, r2, r3 = (r.reshape(BLOCKS, PIVOTS) for r in (r1, r2, r3))
-    g = g.reshape(24, PIVOTS)
-
-    g3 = lax.all_gather(g[12:24], BOTH, axis=1).reshape(3, PIVOTS, PIVOTS)
-    d1 = to_all(g[0:4]).reshape(PIVOTS, PIVOTS)
-    g_next, d1 = after(g[4:12], d1)
-    g2 = to_all(g_next).reshape(2, PIVOTS, PIVOTS)
-    w1 = inverse_factor(d1)
-
-    (h, w1), g2 = after((h, w1), g2)
     cols = lax.all_to_all(h.reshape(COLS, 3, TC, PIVOTS), "col", 0, 0, tiled=True)
-    cols = lax.all_gather(cols.transpose(1, 2, 0, 3), "row", axis=0)
-
-    lp1 = dot_t(g2[1], w1)
-    d2 = g2[0] - dot_t(lp1, lp1)
-    (first, second), d2 = after((first, second), d2)
-    moving = jnp.concatenate([first.transpose(1, 0, 2, 3), second.transpose(1, 0, 2, 3)], axis=1)
+    cols = cols.transpose(1, 2, 0, 3)
+    (first, second), cols = after((first, second), cols)
+    moving = pack(first, second).reshape(TILE, 2 * TR, TC, TILE)
+    (moving, cols), pivot = after((moving, cols), pivot)
+    cols = lax.all_gather(cols, "row", axis=0)
     moving = lax.all_to_all(moving, BOTH, 0, 0, tiled=True)
-    w2 = inverse_factor(d2)
-
-    lp1x = dot_t(g3[0], w1)
-    lp2 = dot_t(g3[1] - dot_t(lp1x, lp1), w2)
-    w3 = inverse_factor(g3[2] - dot_t(lp1x, lp1x) - dot_t(lp2, lp2))
+
+    w1 = inverse_factor(pivot[0])
+    lp1 = dot_t(pivot[2], w1)
+    w2 = inverse_factor(pivot[1] - dot_t(lp1, lp1))
+    lp1x = dot_t(pivot[3], w1)
+    lp2 = dot_t(pivot[4] - dot_t(lp1x, lp1), w2)
+    d3 = pivot[5] - dot_t(lp1x, lp1x) - dot_t(lp2, lp2)
+
+
+    (moving, r1, r2, r3), w2 = after((moving, r1, r2, r3), w2)
+    back = extended(
+        c1,
+        c2,
+        column_masks(c1),
+        column_masks(c2),
+        moving.reshape(ROWS, COLS, 2 * TR, TC, TILE),
+    )
+    back, d3 = after(back, d3)
+    back = lax.all_to_all(back.reshape(128, TR, TC, TILE), BOTH, 0, 0, tiled=True)
+    w3 = inverse_factor(d3)
 
     l1 = dot_t(r1, w1)
     l1x = dot(e1, l1)
@@ -351,30 +424,27 @@
     l2 = dot_t(r2 - dot_t(l1x, lp1), w2)
     l2x = dot(e2, l2)
     l3 = dot_t(r3 - dot_t(l1xx, lp1x) - dot_t(l2x, lp2), w3)
-    rows = jnp.stack([l1, l2, l1xx, l2x, l3]).reshape(5, TR, ROWS, PIVOTS)
-    rows, moving = after(rows, moving)
-    rows = lax.all_to_all(rows.transpose(2, 0, 1, 3), "row", 0, 0, tiled=True)
-    rows = lax.all_gather(rows.transpose(1, 2, 0, 3), "col", axis=0)
-    rows = rows.transpose(1, 2, 3, 0, 4).reshape(5, TR * TILE, PIVOTS)
-
-    back = extended(
-        c1,
-        c2,
-        column_masks(c1),
-        column_masks(c2),
-        moving.reshape(ROWS, COLS, 2 * TR, TC, TILE),
-    )
-    back = lax.all_to_all(back.reshape(128, TR, TC, TILE), BOTH, 0, 0, tiled=True)
+    (l1, l2, l3, cols), back = after((l1, l2, l3, cols), back)
+    cols = cols.transpose(1, 2, 0, 3, 4).reshape(3, TC * TILE, PIVOTS)
+    high = lax.Precision.HIGH
+    l1c = dot_t(cols[0], w1, high)
+    l2c = dot_t(cols[1] - dot_t(l1c, lp1, high), w2, high)
+    l3c = cols[2] - dot_t(l1c, lp1x, high) - dot_t(l2c, lp2, high)
+    l3c = dot_t(l3c, w3, high)
+    rows, (l1, l2, l1c, l2c, l3c) = own_rows(
+        jnp.stack([l1xx, l2x, l3]), (l1, l2, l1c, l2c, l3c)
+    )
+    rows = rows.reshape(3, TR * TILE, PIVOTS)
+    l3r = rows[2]
+    update = (
+        dot_t(rows[0], l1c, high)
+        + dot_t(rows[1], l2c, high)
+        + dot_t(l3r, l3c, high)
+    )
+    outer, update = own_rows(jnp.stack([l1, l2]), update)
+    lower_first, lower_second = outer[0], outer[1]
     assembled = third + back.transpose(1, 0, 2, 3)
 
-    cols = cols.transpose(1, 2, 0, 3, 4).reshape(3, TC * TILE, PIVOTS)
-    l1c = dot_t(cols[0], w1)
-    l2c = dot_t(cols[1] - dot_t(l1c, lp1), w2)
-    l3c = dot_t(cols[2] - dot_t(l1c, lp1x) - dot_t(l2c, lp2), w3)
-    lower_first = rows[0]
-    lower_second = rows[1]
-    l3r = rows[4]
-    update = dot_t(rows[2], l1c) + dot_t(rows[3], l2c) + dot_t(l3r, l3c)
     schur = assembled - update.reshape(TR, TILE, TC, TILE)
     pivot_blocks = PIVOTS // TILE
     row_keep = jnp.arange(TR) * ROWS + lax.axis_index("row") >= pivot_blocks

time: 348 us -> 346 us (level)
  blocking collectives: 38.1 us -> 0 us
  starting transfers between devices: 35.3 us -> 55.3 us
  waiting for transfers between devices: 63.1 us -> 76.9 us
  matrix products: 57.6 us -> 48.3 us
  other arithmetic: 5.18 us -> 9.3 us
  Pallas kernels: 79 us -> 83.1 us
    all_to_all x2 -> x0, blocking collectives: 38.1 us -> none  [the longest x1 24.1 us: per_device(): rows = lax.all_to_all(rows.transpose(2, 0, 1, 3), 'row', 0, 0, tiled=True)]
    all_to_all x3 -> x5, starting transfers between devices: 21.8 us -> 35 us  [the longest x2 14.4 us: own_rows(): lax.all_to_all(many.reshape(ROWS * COLS, n, TR, half), BOTH, 0, 0, tiled=...]
    all_to_all x3 -> x5, waiting for transfers between devices: 47.4 us -> 58.2 us  [the longest x2 20.6 us: own_rows(): lax.all_to_all(many.reshape(ROWS * COLS, n, TR, half), BOTH, 0, 0, tiled=...]
    slice x13 -> x6, local copies, waits for them, and re-layouts: 18.2 us -> 7.52 us  [the longest x2 5.11 us: per_device(): l3c = cols[2] - dot_t(l1c, lp1x, high) - dot_t(l2c, lp2, high)]
    dot_general x22, matrix products: 56.9 us -> 46.2 us  [dot_t(): lax.dot_general(a, b, (((1,), (1,)), ((), ())), precision=precision, pref...]
    transpose x4 -> x2, local copies, waits for them, and re-layouts: 6.49 us -> 0.43 us  [own_rows(): many = rows.reshape(n, TR, ROWS, 2, half).transpose(2, 3, 0, 1, 4)]
    unnamed x65 -> x77, local copies, waits for them, and re-layouts: 11.8 us -> 17.2 us
    concatenate x1 -> x0, local copies, waits for them, and re-layouts: 4.4 us -> none  [per_device(): jnp.concatenate([first.transpose(1, 0, 2, 3), second.transpose(1, 0, 2, 3...]
  transfers between devices with their start and end apart: 8 -> 11, of which waited for: 4 -> 6; matrix products, arithmetic and copies ran while one was open for 27% -> 19% of each run, Pallas kernels for 21% -> 24%
where the time goes in v1:
time: 346 us; the launch traced here: 340 us
  Pallas kernels  83.1 us (24%)
  waiting for transfers between devices  76.9 us (22%)
  starting transfers between devices  55.3 us (16%)
  local copies, waits for them, and re-layouts  52.5 us (15%)
  matrix products  48.3 us (14%)
  between operations  15.1 us (4%)
  other arithmetic  9.3 us (3%)
    pallas_call x3, Pallas kernels, inverse_factor(): pl.pallas_call(chol_kernel, out_shape=jax.ShapeDtypeStruct((PIVOTS, PIVOT...  67.4 us
    dot_general x22, matrix products, dot_t(): lax.dot_general(a, b, (((1,), (1,)), ((), ())), precision=precision, pref...  46.2 us
    all_to_all x2, waiting for transfers between devices, own_rows(): lax.all_to_all(many.reshape(ROWS * COLS, n, TR, half), BOTH, 0, 0, tiled=...  20.6 us
    all_to_all x1, waiting for transfers between devices, per_device(): lax.all_to_all(packed.reshape(128, 16, 128), BOTH, 0, 0, tiled=True)  19.7 us
    all_gather x1, waiting for transfers between devices, per_device(): pivot = lax.all_gather(g, BOTH, axis=1).reshape(6, PIVOTS, PIVOTS)  18.6 us
    unnamed x77, local copies, waits for them, and re-layouts  17.2 us
    all_to_all x2, starting transfers between devices, own_rows(): lax.all_to_all(many.reshape(ROWS * COLS, n, TR, half), BOTH, 0, 0, tiled=...  14.4 us
    all_to_all x1, starting transfers between devices, per_device(): top = lax.all_to_all(packed[:, 0], BOTH, 0, 0, tiled=True)  11.5 us
  transfers between devices with their start and end apart: 11, of which 6 were waited for; matrix products, arithmetic and copies ran while one was open for 19% of the time, Pallas kernels for 24%

profile of v1, /device:TPU:1, one launch (start us, length us, event | category | flops | bytes accessed | tf_op | source)
XLA Modules:
  0.0 340.3 jit_solution(12403646603524594449)
XLA Ops:
  13.8 11.5 %all-to-all-start = ((f32[128,4,128]{2,1,0:T(4,128)}), f32[128,4,128]{2,1,0:T(4,128)S(1)}, u32[]{:S(2)}, u32[]{:S(2)}) async-start(f32[128,4,128]{2,1,0:T(4,128)} %slice_bitcast_fusion.1), calls=%async_computation | async-start | bytes 524288 | tf_op jit(solution)/shard_map/all_to_all | solution.py:385
  25.5 10.7 %all-to-all-done = f32[128,4,128]{2,1,0:T(4,128)S(1)} async-done(((f32[128,4,128]{2,1,0:T(4,128)}), f32[128,4,128]{2,1,0:T(4,128)S(1)}, u32[]{:S(2)}, u32[]{:S(2)}) %all-to-all-start) | async-done | bytes 262176 | tf_op jit(solution)/shard_map/all_to_all | solution.py:385
  40.0 4.7 %all-to-all-start.1 = ((f32[128,16,128]{2,1,0:T(8,128)}), f32[128,16,128]{2,1,0:T(8,128)S(1)}, u32[]{:S(2)}, u32[]{:S(2)}) async-start(f32[128,16,128]{2,1,0:T(8,128)} %copy.62), calls=%async_computation.1 | async-start | bytes 2097152 | tf_op jit(solution)/shard_map/all_to_all | solution.py:390
  44.8 19.7 %all-to-all-done.1 = f32[128,16,128]{2,1,0:T(8,128)S(1)} async-done(((f32[128,16,128]{2,1,0:T(8,128)}), f32[128,16,128]{2,1,0:T(8,128)S(1)}, u32[]{:S(2)}, u32[]{:S(2)}) %all-to-all-start.1) | async-done | bytes 1048608 | tf_op jit(solution)/shard_map/all_to_all | solution.py:390
  64.5 7.3 %shard_map.85 = (f32[64,4,128]{2,1,0:T(4,128)S(1)}, f32[64,4,128]{2,1,0:T(4,128)S(1)}, f32[64,4,128]{2,1,0:T(4,128)S(1)}, f32[8,3,8,4,128]{4,3,2,1,0:T(4,128)S(1)}) custom-call(s32[64]{0:T(128)S(1)} %get-tuple-element.106.c1_ref, s32[64]{0:T(128)S(1)} %get-tuple-element.107.c2_ref, f32[16,8,16,128]{3,2,1,0:T(8,128)S(1)} %bitcast.139), custom_call_target="tpu_custom_call" | custom-call | tf_op jit(solution)/shard_map/pallas_call | solution.py:235
  74.7 4.5 %all-to-all-start.2 = ((f32[8,3,8,512]{3,2,1,0:T(8,128)}), f32[8,3,8,512]{3,2,1,0:T(8,128)S(1)}, u32[]{:S(2)}, u32[]{:S(2)}) async-start(f32[8,3,8,512]{3,2,1,0:T(8,128)} %reshape.312), calls=%async_computation.2 | async-start | bytes 786432 | tf_op jit(solution)/shard_map/all_to_all | solution.py:393
  80.5 7.2 %all-to-all-done.2 = f32[8,3,8,512]{3,2,1,0:T(8,128)S(1)} async-done(((f32[8,3,8,512]{3,2,1,0:T(8,128)}), f32[8,3,8,512]{3,2,1,0:T(8,128)S(1)}, u32[]{:S(2)}, u32[]{:S(2)}) %all-to-all-start.2) | async-done | bytes 393248 | tf_op jit(solution)/shard_map/all_to_all | solution.py:393
  92.2 18.6 %all-gather.5.cloned.1.call-done = f32[24,65536]{1,0:T(8,128)} async-done(((f32[24,512]{1,0:T(8,128)}), f32[24,65536]{1,0:T(8,128)}) %all-gather.5.cloned.1.call-update) | async-done | bytes 6291472 | tf_op jit(solution)/shard_map/all_gather | solution.py:388
  110.8 6.9 %reshape.314 = f32[6,512,512]{2,1,0:T(8,128)} reshape(f32[24,65536]{1,0:T(8,128)} %all-gather.5.cloned.1.call-done) | data formatting | bytes 12582912 | tf_op jit(solution)/shard_map/reshape | solution.py:388
  120.2 7.0 %all-to-all-start.3 = ((f32[128,8,8,128]{3,2,1,0:T(8,128)}), f32[128,8,8,128]{3,2,1,0:T(8,128)}, u32[]{:S(2)}, u32[]{:S(2)}) async-start(f32[128,8,8,128]{3,2,1,0:T(8,128)} %bitcast.137), calls=%async_computation.3 | async-start | bytes 8388608 | tf_op jit(solution)/shard_map/all_to_all | solution.py:399
  128.7 22.4 %shard_map.87 = f32[512,512]{1,0:T(8,128)S(1)} custom-call(f32[512,512]{1,0:T(8,128)S(1)} %slice_bitcast_fusion.d_ref), custom_call_target="tpu_custom_call" | custom-call | flops 24999999488 | bytes 2000000 | tf_op jit(solution)/shard_map/pallas_call | solution.py:135
  158.6 22.6 %shard_map.88 = f32[512,512]{1,0:T(8,128)S(1)} custom-call(f32[512,512]{1,0:T(8,128)S(1)} %convolution_subtract_fusion.3.d_ref), custom_call_target="tpu_custom_call" | custom-call | flops 24999999488 | bytes 2000000 | tf_op jit(solution)/shard_map/pallas_call | solution.py:135
  188.1 6.2 %shard_map.89 = f32[16,8,4,8,128]{4,3,2,1,0:T(8,128)S(1)} custom-call(s32[64]{0:T(128)S(1)} %get-tuple-element.106.c1_ref, s32[64]{0:T(128)S(1)} %get-tuple-element.107.c2_ref, f32[5,8,8,128]{3,2,1,0:T(8,128)S(1)} %broadcast_in_dim.36.m1_ref, f32[5,8,8,128]{3,2,1,0:T(8,128)S(1)} %broadcast_in_dim.37.m2_ref, f32[16,8,8,8,128]{4,3,2,1,0:T(8,128)} %bitcast.17.a_ref), custom_call_target="tpu_custom_call" | custom-call | tf_op jit(solution)/shard_map/pallas_call | solution.py:316
  195.7 10.7 %all-to-all-start.4 = ((f32[128,4,8,128]{3,2,1,0:T(8,128)}), f32[128,4,8,128]{3,2,1,0:T(8,128)}, u32[]{:S(2)}, u32[]{:S(2)}) async-start(f32[128,4,8,128]{3,2,1,0:T(8,128)} %bitcast.138), calls=%async_computation.4 | async-start | bytes 4194304 | tf_op jit(solution)/shard_map/all_to_all | solution.py:418
  221.7 22.4 %shard_map.90 = f32[512,512]{1,0:T(8,128)S(1)} custom-call(f32[512,512]{1,0:T(8,128)S(1)} %copy-done.4), custom_call_target="tpu_custom_call" | custom-call | flops 24999999488 | bytes 2000000 | tf_op jit(solution)/shard_map/pallas_call | solution.py:135
  245.2 3.6 %fusion.29 = (f32[1,8,16,8,512]{4,3,1,0,2:T(8,128)S(1)}, f32[1,8,16,8,512]{4,3,1,0,2:T(8,128)S(1)}, f32[1,8,16,8,512]{4,3,1,0,2:T(8,128)S(1)}) fusion(f32[3,8,16,8,512]{4,3,1,0,2:T(8,128)} %bitcast.154), kind=kLoop, calls=%fused_computation.81 | loop fusion | bytes 12582912 | tf_op jit(solution)/shard_map/slice | solution.py:432
  250.9 3.2 fusion.38
  259.2 10.5 %all-to-all-start.5 = ((f32[128,3,4,256]{3,2,1,0:T(4,128)}), f32[128,3,4,256]{3,2,1,0:T(4,128)}, u32[]{:S(2)}, u32[]{:S(2)}) async-start(f32[128,3,4,256]{3,2,1,0:T(4,128)} %bitcast.155), calls=%async_computation.5 | async-start | bytes 3145728 | tf_op jit(solution)/shard_map/all_to_all | solution.py:359
  269.7 4.2 %bitcast_subtract_fusion.2 = f32[1024,512]{1,0:T(8,128)S(1)} fusion(f32[1,8,16,8,512]{4,3,2,1,0:T(8,128)} %copy.68, f32[1024,512]{1,0:T(8,128)} %copy-done.15, f32[512,512]{1,0:T(8,128)S(1)} %copy-done.12), kind=kOutput, calls=%fused_computation.8 | convolution fusion | flops 1611137024 | bytes 7340032 | tf_op jit(solution)/shard_map/dot_general | solution.py:331
  280.5 13.5 %all-to-all-done.5 = f32[128,3,4,256]{3,2,1,0:T(4,128)} async-done(((f32[128,3,4,256]{3,2,1,0:T(4,128)}), f32[128,3,4,256]{3,2,1,0:T(4,128)}, u32[]{:S(2)}, u32[]{:S(2)}) %all-to-all-start.5) | async-done | bytes 1572896 | tf_op jit(solution)/shard_map/all_to_all | solution.py:359
  299.8 3.8 %all-to-all-start.6 = ((f32[128,2,4,256]{3,2,1,0:T(4,128)}), f32[128,2,4,256]{3,2,1,0:T(4,128)S(1)}, u32[]{:S(2)}, u32[]{:S(2)}) async-start(f32[128,2,4,256]{3,2,1,0:T(4,128)} %bitcast.157), calls=%async_computation.6 | async-start | bytes 2097152 | tf_op jit(solution)/shard_map/all_to_all | solution.py:359
  312.2 3.4 %add_add_fusion = f32[512,1024]{1,0:T(8,128)} fusion(f32[512,1024]{1,0:T(8,128)S(1)} %fusion.40, f32[512,1024]{1,0:T(8,128)S(1)} %fusion.41, f32[512,512]{1,0:T(8,128)S(1)} %bitcast.158, f32[1024,512]{1,0:T(8,128)S(1)} %fusion.39), kind=kOutput, calls=%fused_computation.9 | convolution fusion | flops 1611661312 | bytes 9437184 | tf_op jit(solution)/shard_map/dot_general | solution.py:331
  315.6 7.1 %all-to-all-done.6 = f32[128,2,4,256]{3,2,1,0:T(4,128)S(1)} async-done(((f32[128,2,4,256]{3,2,1,0:T(4,128)}), f32[128,2,4,256]{3,2,1,0:T(4,128)S(1)}, u32[]{:S(2)}, u32[]{:S(2)}) %all-to-all-start.6) | async-done | bytes 1048608 | tf_op jit(solution)/shard_map/all_to_all | solution.py:359
  326.3 3.2 fusion.1
  (168 shorter events, 90.2 us)
Async XLA Ops:
  8.9 16.5 %copy-start.31 = (s32[60]{0:T(128)S(1)}, s32[60]{0:T(128)}, u32[]{:S(2)}) copy-start(s32[60]{0:T(128)} %param.9) | copy-start | bytes 724
  8.9 16.5 %copy-start.32 = (s32[60]{0:T(128)S(1)}, s32[60]{0:T(128)}, u32[]{:S(2)}) copy-start(s32[60]{0:T(128)} %param.8) | copy-start | bytes 724
  13.8 22.4 %all-to-all-start = ((f32[128,4,128]{2,1,0:T(4,128)}), f32[128,4,128]{2,1,0:T(4,128)S(1)}, u32[]{:S(2)}, u32[]{:S(2)}) async-start(f32[128,4,128]{2,1,0:T(4,128)} %slice_bitcast_fusion.1), calls=%async_computation | async-start | bytes 524288 | tf_op jit(solution)/shard_map/all_to_all | solution.py:385
  25.3 85.5 %all-gather.5.cloned.1.call-start = ((), (), s32[]{:S(2)}) async-start(), calls=%async_computation.7 | async-start | bytes 6340608 | tf_op jit(solution)/shard_map/all_gather | solution.py:388
  40.0 47.7 %copy-start.2 = (f32[1,4,128,1,8,128]{5,4,3,2,1,0:T(8,128)S(1)}, f32[1,4,128,1,8,128]{5,4,3,2,1,0:T(8,128)}, u32[]{:S(2)}) copy-start(f32[1,4,128,1,8,128]{5,4,3,2,1,0:T(8,128)} %param.5) | copy-start | bytes 6291460
  40.0 24.5 %all-to-all-start.1 = ((f32[128,16,128]{2,1,0:T(8,128)}), f32[128,16,128]{2,1,0:T(8,128)S(1)}, u32[]{:S(2)}, u32[]{:S(2)}) async-start(f32[128,16,128]{2,1,0:T(8,128)} %copy.62), calls=%async_computation.1 | async-start | bytes 2097152 | tf_op jit(solution)/shard_map/all_to_all | solution.py:390
  44.7 19.8 %copy-start.28 = (pred[5,8,8]{2,1,0:T(8,128)(4,1)}, pred[5,8,8]{2,1,0:T(8,128)(4,1)S(1)}, u32[]{:S(2)}) copy-start(pred[5,8,8]{2,1,0:T(8,128)(4,1)S(1)} %constant_dynamic-update-slice_fusion.5) | copy-start | bytes 964
  44.8 19.7 %copy-start.29 = (pred[5,8,8]{2,1,0:T(8,128)(4,1)}, pred[5,8,8]{2,1,0:T(8,128)(4,1)S(1)}, u32[]{:S(2)}) copy-start(pred[5,8,8]{2,1,0:T(8,128)(4,1)S(1)} %constant_dynamic-update-slice_fusion.1) | copy-start | bytes 964
  74.7 13.0 %all-to-all-start.2 = ((f32[8,3,8,512]{3,2,1,0:T(8,128)}), f32[8,3,8,512]{3,2,1,0:T(8,128)S(1)}, u32[]{:S(2)}, u32[]{:S(2)}) async-start(f32[8,3,8,512]{3,2,1,0:T(8,128)} %reshape.312), calls=%async_computation.2 | async-start | bytes 786432 | tf_op jit(solution)/shard_map/all_to_all | solution.py:393
  79.3 165.9 %all-gather.7.cloned.1.call-start = ((), (), s32[]{:S(2)}) async-start(), calls=%async_computation.8 | async-start | bytes 6684672 | tf_op jit(solution)/shard_map/all_gather | solution.py:398
  92.2 26.5 %copy-start.30 = (pred[5,8,8]{2,1,0:T(8,128)(4,1)S(1)}, pred[5,8,8]{2,1,0:T(8,128)(4,1)}, u32[]{:S(2)}) copy-start(pred[5,8,8]{2,1,0:T(8,128)(4,1)} %constant_dynamic-update-slice_fusion) | copy-start | bytes 964
  92.2 26.7 %copy-start.10 = (f32[64,4,128]{2,1,0:T(4,128)S(1)}, f32[64,4,128]{2,1,0:T(4,128)}, u32[]{:S(2)}) copy-start(f32[64,4,128]{2,1,0:T(4,128)} %copy-done.9) | copy-start | bytes 393220
  92.2 27.4 %copy-start.8 = (f32[64,4,128]{2,1,0:T(4,128)S(1)}, f32[64,4,128]{2,1,0:T(4,128)}, u32[]{:S(2)}) copy-start(f32[64,4,128]{2,1,0:T(4,128)} %copy-done.7) | copy-start | bytes 393220
  92.2 28.0 %copy-start.6 = (f32[64,4,128]{2,1,0:T(4,128)S(1)}, f32[64,4,128]{2,1,0:T(4,128)}, u32[]{:S(2)}) copy-start(f32[64,4,128]{2,1,0:T(4,128)} %copy-done.5) | copy-start | bytes 393220
  120.2 67.7 %all-to-all-start.3 = ((f32[128,8,8,128]{3,2,1,0:T(8,128)}), f32[128,8,8,128]{3,2,1,0:T(8,128)}, u32[]{:S(2)}, u32[]{:S(2)}) async-start(f32[128,8,8,128]{3,2,1,0:T(8,128)} %bitcast.137), calls=%async_computation.3 | async-start | bytes 8388608 | tf_op jit(solution)/shard_map/all_to_all | solution.py:399
  127.2 23.8 %slice-start = ((s8[6291456]{0:T(1024)(128)(4,1)}), s8[4194304]{0:T(1024)(128)(4,1)S(1)}, s32[]{:S(2)}) async-start(s8[6291456]{0:T(1024)(128)(4,1)} %bitcast.149), calls=%async_computation.9 | async-start | bytes 8388608
  128.7 22.4 %slice-start.1 = ((s8[6291456]{0:T(1024)(128)(4,1)}), s8[2097152]{0:T(1024)(128)(4,1)S(1)}, s32[]{:S(2)}) async-start(s8[6291456]{0:T(1024)(128)(4,1)} %bitcast.149), calls=%async_computation.10 | async-start | bytes 4194304
  153.0 30.2 %copy-start.13 = (f32[512,512]{1,0:T(8,128)}, f32[512,512]{1,0:T(8,128)S(1)}, u32[]{:S(2)}) copy-start(f32[512,512]{1,0:T(8,128)S(1)} %fusion.3) | copy-start | bytes 3145732
  154.9 52.9 %copy-start.11 = (f32[512,512]{1,0:T(8,128)}, f32[512,512]{1,0:T(8,128)S(1)}, u32[]{:S(2)}) copy-start(f32[512,512]{1,0:T(8,128)S(1)} %fusion.5) | copy-start | bytes 3145732
  195.7 49.5 %all-to-all-start.4 = ((f32[128,4,8,128]{3,2,1,0:T(8,128)}), f32[128,4,8,128]{3,2,1,0:T(8,128)}, u32[]{:S(2)}, u32[]{:S(2)}) async-start(f32[128,4,8,128]{3,2,1,0:T(8,128)} %bitcast.138), calls=%async_computation.4 | async-start | bytes 4194304 | tf_op jit(solution)/shard_map/all_to_all | solution.py:418
  259.2 34.8 %all-to-all-start.5 = ((f32[128,3,4,256]{3,2,1,0:T(4,128)}), f32[128,3,4,256]{3,2,1,0:T(4,128)}, u32[]{:S(2)}, u32[]{:S(2)}) async-start(f32[128,3,4,256]{3,2,1,0:T(4,128)} %bitcast.155), calls=%async_computation.5 | async-start | bytes 3145728 | tf_op jit(solution)/shard_map/all_to_all | solution.py:359
  296.8 6.8 %collective-permute-start = (f32[128,3,4,256]{3,0,2,1:T(8,128)}, f32[128,3,4,256]{3,0,2,1:T(8,128)}, u32[]{:S(2)}, u32[]{:S(2)}) collective-permute-start(f32[128,3,4,256]{3,0,2,1:T(8,128)} %copy.72), channel_id=1, source_target_pairs={{0,1},{1,0},{2,3},{3,2},{4,5},{5,4},{6,7},{7,6},{8,9},{9,8},{10,11... | collective-permute-start | bytes 4718600 | tf_op jit(solution)/shard_map/ppermute | solution.py:363
  299.8 23.0 %all-to-all-start.6 = ((f32[128,2,4,256]{3,2,1,0:T(4,128)}), f32[128,2,4,256]{3,2,1,0:T(4,128)S(1)}, u32[]{:S(2)}, u32[]{:S(2)}) async-start(f32[128,2,4,256]{3,2,1,0:T(4,128)} %bitcast.157), calls=%async_computation.6 | async-start | bytes 2097152 | tf_op jit(solution)/shard_map/all_to_all | solution.py:359
  322.8 6.8 %collective-permute-start.1 = (f32[128,2,4,256]{3,2,1,0:T(4,128)S(1)}, f32[128,2,4,256]{3,2,1,0:T(4,128)S(1)}, u32[]{:S(2)}, u32[]{:S(2)}) collective-permute-start(f32[128,2,4,256]{3,2,1,0:T(4,128)S(1)} %all-to-all-done.6), channel_id=1, source_target_pairs={{0,1},{1,0},{2,3},{3,2},{4,5},{5,4},{6,7},{7,6},{8,9},{9,8},{10,11... | collective-permute-start | bytes 3145736 | tf_op jit(solution)/shard_map/ppermute | solution.py:363
  (22 other events, 59.0 us)
Sparse Core Ops, SparseCore 0:
  38.2 72.5 all-gather.4
  118.8 116.4 all-gather.6

commit v2 on v1

--- a/solution.py
+++ b/solution.py
@@ -441,8 +441,6 @@
         + dot_t(rows[1], l2c, high)
         + dot_t(l3r, l3c, high)
     )
-    outer, update = own_rows(jnp.stack([l1, l2]), update)
-    lower_first, lower_second = outer[0], outer[1]
     assembled = third + back.transpose(1, 0, 2, 3)
 
     schur = assembled - update.reshape(TR, TILE, TC, TILE)
@@ -451,6 +449,8 @@
     col_keep = jnp.arange(TC) * COLS + lax.axis_index("col") >= pivot_blocks
     keep = row_keep[:, None, None, None] & col_keep[None, None, :, None]
     schur = jnp.where(keep, schur, 0.0)
+    outer, schur = own_rows(jnp.stack([l1, l2]), schur)
+    lower_first, lower_second = outer[0], outer[1]
     out = (1, TR, TILE, PIVOTS)
     return (
         lower_first.reshape(out),

time: 346 us -> 343 us (level)
    all_to_all x2, waiting for transfers between devices: 20.6 us -> 17 us  [own_rows(): lax.all_to_all(many.reshape(ROWS * COLS, n, TR, half), BOTH, 0, 0, tiled=...]
  transfers between devices with their start and end apart: 11 -> 11, of which waited for: 6 -> 7; matrix products, arithmetic and copies ran while one was open for 19% -> 18% of each run, Pallas kernels for 24% -> 24%
where the time goes in v2:
time: 343 us; the launch traced here: 337 us
  Pallas kernels  83.1 us (24%)
  waiting for transfers between devices  75.5 us (22%)
  starting transfers between devices  55.3 us (16%)
  local copies, waits for them, and re-layouts  51.8 us (15%)
  matrix products  46.9 us (14%)
  between operations  15.1 us (4%)
  other arithmetic  9.45 us (3%)
    pallas_call x3, Pallas kernels, inverse_factor(): pl.pallas_call(chol_kernel, out_shape=jax.ShapeDtypeStruct((PIVOTS, PIVOT...  67.4 us
    dot_general x22, matrix products, dot_t(): lax.dot_general(a, b, (((1,), (1,)), ((), ())), precision=precision, pref...  44.9 us
    all_to_all x1, waiting for transfers between devices, per_device(): lax.all_to_all(packed.reshape(128, 16, 128), BOTH, 0, 0, tiled=True)  19.7 us
    all_gather x1, waiting for transfers between devices, per_device(): pivot = lax.all_gather(g, BOTH, axis=1).reshape(6, PIVOTS, PIVOTS)  18.6 us
    all_to_all x2, waiting for transfers between devices, own_rows(): lax.all_to_all(many.reshape(ROWS * COLS, n, TR, half), BOTH, 0, 0, tiled=...  17 us
    unnamed x77, local copies, waits for them, and re-layouts  16.5 us
    all_to_all x2, starting transfers between devices, own_rows(): lax.all_to_all(many.reshape(ROWS * COLS, n, TR, half), BOTH, 0, 0, tiled=...  14.4 us
    all_to_all x1, starting transfers between devices, per_device(): top = lax.all_to_all(packed[:, 0], BOTH, 0, 0, tiled=True)  11.5 us
  transfers between devices with their start and end apart: 11, of which 7 were waited for; matrix products, arithmetic and copies ran while one was open for 18% of the time, Pallas kernels for 24%

profile of v2, /device:TPU:1, one launch (start us, length us, event | category | flops | bytes accessed | tf_op | source)
XLA Modules:
  0.0 337.1 jit_solution(16766392482361480074)
XLA Ops:
  13.8 11.5 %all-to-all-start = ((f32[128,4,128]{2,1,0:T(4,128)}), f32[128,4,128]{2,1,0:T(4,128)S(1)}, u32[]{:S(2)}, u32[]{:S(2)}) async-start(f32[128,4,128]{2,1,0:T(4,128)} %slice_bitcast_fusion.1), calls=%async_computation | async-start | bytes 524288 | tf_op jit(solution)/shard_map/all_to_all | solution.py:385
  25.5 10.7 %all-to-all-done = f32[128,4,128]{2,1,0:T(4,128)S(1)} async-done(((f32[128,4,128]{2,1,0:T(4,128)}), f32[128,4,128]{2,1,0:T(4,128)S(1)}, u32[]{:S(2)}, u32[]{:S(2)}) %all-to-all-start) | async-done | bytes 262176 | tf_op jit(solution)/shard_map/all_to_all | solution.py:385
  40.0 4.7 %all-to-all-start.1 = ((f32[128,16,128]{2,1,0:T(8,128)}), f32[128,16,128]{2,1,0:T(8,128)S(1)}, u32[]{:S(2)}, u32[]{:S(2)}) async-start(f32[128,16,128]{2,1,0:T(8,128)} %copy.62), calls=%async_computation.1 | async-start | bytes 2097152 | tf_op jit(solution)/shard_map/all_to_all | solution.py:390
  44.8 19.7 %all-to-all-done.1 = f32[128,16,128]{2,1,0:T(8,128)S(1)} async-done(((f32[128,16,128]{2,1,0:T(8,128)}), f32[128,16,128]{2,1,0:T(8,128)S(1)}, u32[]{:S(2)}, u32[]{:S(2)}) %all-to-all-start.1) | async-done | bytes 1048608 | tf_op jit(solution)/shard_map/all_to_all | solution.py:390
  64.5 7.3 %shard_map.85 = (f32[64,4,128]{2,1,0:T(4,128)S(1)}, f32[64,4,128]{2,1,0:T(4,128)S(1)}, f32[64,4,128]{2,1,0:T(4,128)S(1)}, f32[8,3,8,4,128]{4,3,2,1,0:T(4,128)S(1)}) custom-call(s32[64]{0:T(128)S(1)} %get-tuple-element.106.c1_ref, s32[64]{0:T(128)S(1)} %get-tuple-element.107.c2_ref, f32[16,8,16,128]{3,2,1,0:T(8,128)S(1)} %bitcast.137), custom_call_target="tpu_custom_call" | custom-call | tf_op jit(solution)/shard_map/pallas_call | solution.py:235
  74.7 4.5 %all-to-all-start.2 = ((f32[8,3,8,512]{3,2,1,0:T(8,128)}), f32[8,3,8,512]{3,2,1,0:T(8,128)S(1)}, u32[]{:S(2)}, u32[]{:S(2)}) async-start(f32[8,3,8,512]{3,2,1,0:T(8,128)} %reshape.312), calls=%async_computation.2 | async-start | bytes 786432 | tf_op jit(solution)/shard_map/all_to_all | solution.py:393
  80.5 7.2 %all-to-all-done.2 = f32[8,3,8,512]{3,2,1,0:T(8,128)S(1)} async-done(((f32[8,3,8,512]{3,2,1,0:T(8,128)}), f32[8,3,8,512]{3,2,1,0:T(8,128)S(1)}, u32[]{:S(2)}, u32[]{:S(2)}) %all-to-all-start.2) | async-done | bytes 393248 | tf_op jit(solution)/shard_map/all_to_all | solution.py:393
  92.2 18.6 %all-gather.5.cloned.1.call-done = f32[24,65536]{1,0:T(8,128)} async-done(((f32[24,512]{1,0:T(8,128)}), f32[24,65536]{1,0:T(8,128)}) %all-gather.5.cloned.1.call-update) | async-done | bytes 6291472 | tf_op jit(solution)/shard_map/all_gather | solution.py:388
  110.8 6.9 %reshape.314 = f32[6,512,512]{2,1,0:T(8,128)} reshape(f32[24,65536]{1,0:T(8,128)} %all-gather.5.cloned.1.call-done) | data formatting | bytes 12582912 | tf_op jit(solution)/shard_map/reshape | solution.py:388
  120.2 7.0 %all-to-all-start.3 = ((f32[128,8,8,128]{3,2,1,0:T(8,128)}), f32[128,8,8,128]{3,2,1,0:T(8,128)}, u32[]{:S(2)}, u32[]{:S(2)}) async-start(f32[128,8,8,128]{3,2,1,0:T(8,128)} %bitcast.135), calls=%async_computation.3 | async-start | bytes 8388608 | tf_op jit(solution)/shard_map/all_to_all | solution.py:399
  128.7 22.4 %shard_map.87 = f32[512,512]{1,0:T(8,128)S(1)} custom-call(f32[512,512]{1,0:T(8,128)S(1)} %slice_bitcast_fusion.d_ref), custom_call_target="tpu_custom_call" | custom-call | flops 24999999488 | bytes 2000000 | tf_op jit(solution)/shard_map/pallas_call | solution.py:135
  158.6 22.6 %shard_map.88 = f32[512,512]{1,0:T(8,128)S(1)} custom-call(f32[512,512]{1,0:T(8,128)S(1)} %convolution_subtract_fusion.3.d_ref), custom_call_target="tpu_custom_call" | custom-call | flops 24999999488 | bytes 2000000 | tf_op jit(solution)/shard_map/pallas_call | solution.py:135
  188.1 6.2 %shard_map.89 = f32[16,8,4,8,128]{4,3,2,1,0:T(8,128)S(1)} custom-call(s32[64]{0:T(128)S(1)} %get-tuple-element.106.c1_ref, s32[64]{0:T(128)S(1)} %get-tuple-element.107.c2_ref, f32[5,8,8,128]{3,2,1,0:T(8,128)S(1)} %broadcast_in_dim.40.m1_ref, f32[5,8,8,128]{3,2,1,0:T(8,128)S(1)} %broadcast_in_dim.41.m2_ref, f32[16,8,8,8,128]{4,3,2,1,0:T(8,128)} %bitcast.17.a_ref), custom_call_target="tpu_custom_call" | custom-call | tf_op jit(solution)/shard_map/pallas_call | solution.py:316
  195.7 10.7 %all-to-all-start.4 = ((f32[128,4,8,128]{3,2,1,0:T(8,128)}), f32[128,4,8,128]{3,2,1,0:T(8,128)}, u32[]{:S(2)}, u32[]{:S(2)}) async-start(f32[128,4,8,128]{3,2,1,0:T(8,128)} %bitcast.136), calls=%async_computation.4 | async-start | bytes 4194304 | tf_op jit(solution)/shard_map/all_to_all | solution.py:418
  221.7 22.4 %shard_map.90 = f32[512,512]{1,0:T(8,128)S(1)} custom-call(f32[512,512]{1,0:T(8,128)S(1)} %copy-done.4), custom_call_target="tpu_custom_call" | custom-call | flops 24999999488 | bytes 2000000 | tf_op jit(solution)/shard_map/pallas_call | solution.py:135
  245.2 3.6 %fusion.28 = (f32[1,8,16,8,512]{4,3,1,0,2:T(8,128)S(1)}, f32[1,8,16,8,512]{4,3,1,0,2:T(8,128)S(1)}, f32[1,8,16,8,512]{4,3,1,0,2:T(8,128)S(1)}) fusion(f32[3,8,16,8,512]{4,3,1,0,2:T(8,128)} %bitcast.151), kind=kLoop, calls=%fused_computation.80 | loop fusion | bytes 12582912 | tf_op jit(solution)/shard_map/slice | solution.py:432
  250.9 3.2 fusion.37
  259.2 10.5 %all-to-all-start.5 = ((f32[128,3,4,256]{3,2,1,0:T(4,128)}), f32[128,3,4,256]{3,2,1,0:T(4,128)}, u32[]{:S(2)}, u32[]{:S(2)}) async-start(f32[128,3,4,256]{3,2,1,0:T(4,128)} %bitcast.152), calls=%async_computation.5 | async-start | bytes 3145728 | tf_op jit(solution)/shard_map/all_to_all | solution.py:359
  269.7 4.2 %bitcast_subtract_fusion.2 = f32[1024,512]{1,0:T(8,128)S(1)} fusion(f32[1,8,16,8,512]{4,3,2,1,0:T(8,128)} %copy.68, f32[1024,512]{1,0:T(8,128)} %copy-done.15, f32[512,512]{1,0:T(8,128)S(1)} %copy-done.12), kind=kOutput, calls=%fused_computation.7 | convolution fusion | flops 1611137024 | bytes 7340032 | tf_op jit(solution)/shard_map/dot_general | solution.py:331
  280.5 13.5 %all-to-all-done.5 = f32[128,3,4,256]{3,2,1,0:T(4,128)} async-done(((f32[128,3,4,256]{3,2,1,0:T(4,128)}), f32[128,3,4,256]{3,2,1,0:T(4,128)}, u32[]{:S(2)}, u32[]{:S(2)}) %all-to-all-start.5) | async-done | bytes 1572896 | tf_op jit(solution)/shard_map/all_to_all | solution.py:359
  294.0 2.9 copy.73
  299.9 3.8 %all-to-all-start.6 = ((f32[128,2,4,256]{3,2,1,0:T(4,128)}), f32[128,2,4,256]{3,2,1,0:T(4,128)S(1)}, u32[]{:S(2)}, u32[]{:S(2)}) async-start(f32[128,2,4,256]{3,2,1,0:T(4,128)} %bitcast.154), calls=%async_computation.6 | async-start | bytes 2097152 | tf_op jit(solution)/shard_map/all_to_all | solution.py:359
  316.0 3.4 %fusion = f32[4,128,8,128]{3,2,1,0:T(8,128)} fusion(f32[128,4,8,128]{3,2,1,0:T(8,128)} %all-to-all-done.4, pred[4,8]{1,0:T(4,128)(4,1)S(1)} %broadcast_and_fusion, f32[1,4,128,1,8,128]{5,4,3,2,1,0:T(8,128)S(1)} %copy-done.25, f32[4,128,8,128]{3,2,1,0:T(8,128)S(1)} %bitcast.150), kind=kLoop, calls=%fused_computation.2 | loop fusion | flops 1572864 | bytes 8388640 | tf_op jit(solution)/shard_map/jit(_where)/select_n | solution.py:451
  319.3 3.5 %all-to-all-done.6 = f32[128,2,4,256]{3,2,1,0:T(4,128)S(1)} async-done(((f32[128,2,4,256]{3,2,1,0:T(4,128)}), f32[128,2,4,256]{3,2,1,0:T(4,128)S(1)}, u32[]{:S(2)}, u32[]{:S(2)}) %all-to-all-start.6) | async-done | bytes 1048608 | tf_op jit(solution)/shard_map/all_to_all | solution.py:359
  (168 shorter events, 91.0 us)
Async XLA Ops:
  8.9 16.5 %copy-start.31 = (s32[60]{0:T(128)S(1)}, s32[60]{0:T(128)}, u32[]{:S(2)}) copy-start(s32[60]{0:T(128)} %param.9) | copy-start | bytes 724
  8.9 16.5 %copy-start.32 = (s32[60]{0:T(128)S(1)}, s32[60]{0:T(128)}, u32[]{:S(2)}) copy-start(s32[60]{0:T(128)} %param.8) | copy-start | bytes 724
  13.8 22.4 %all-to-all-start = ((f32[128,4,128]{2,1,0:T(4,128)}), f32[128,4,128]{2,1,0:T(4,128)S(1)}, u32[]{:S(2)}, u32[]{:S(2)}) async-start(f32[128,4,128]{2,1,0:T(4,128)} %slice_bitcast_fusion.1), calls=%async_computation | async-start | bytes 524288 | tf_op jit(solution)/shard_map/all_to_all | solution.py:385
  25.3 85.5 %all-gather.5.cloned.1.call-start = ((), (), s32[]{:S(2)}) async-start(), calls=%async_computation.7 | async-start | bytes 6340608 | tf_op jit(solution)/shard_map/all_gather | solution.py:388
  40.0 47.7 %copy-start.2 = (f32[1,4,128,1,8,128]{5,4,3,2,1,0:T(8,128)S(1)}, f32[1,4,128,1,8,128]{5,4,3,2,1,0:T(8,128)}, u32[]{:S(2)}) copy-start(f32[1,4,128,1,8,128]{5,4,3,2,1,0:T(8,128)} %param.5) | copy-start | bytes 6291460
  40.0 24.5 %all-to-all-start.1 = ((f32[128,16,128]{2,1,0:T(8,128)}), f32[128,16,128]{2,1,0:T(8,128)S(1)}, u32[]{:S(2)}, u32[]{:S(2)}) async-start(f32[128,16,128]{2,1,0:T(8,128)} %copy.62), calls=%async_computation.1 | async-start | bytes 2097152 | tf_op jit(solution)/shard_map/all_to_all | solution.py:390
  44.7 19.8 %copy-start.28 = (pred[5,8,8]{2,1,0:T(8,128)(4,1)}, pred[5,8,8]{2,1,0:T(8,128)(4,1)S(1)}, u32[]{:S(2)}) copy-start(pred[5,8,8]{2,1,0:T(8,128)(4,1)S(1)} %constant_dynamic-update-slice_fusion.5) | copy-start | bytes 964
  44.8 19.7 %copy-start.29 = (pred[5,8,8]{2,1,0:T(8,128)(4,1)}, pred[5,8,8]{2,1,0:T(8,128)(4,1)S(1)}, u32[]{:S(2)}) copy-start(pred[5,8,8]{2,1,0:T(8,128)(4,1)S(1)} %constant_dynamic-update-slice_fusion.1) | copy-start | bytes 964
  74.7 13.0 %all-to-all-start.2 = ((f32[8,3,8,512]{3,2,1,0:T(8,128)}), f32[8,3,8,512]{3,2,1,0:T(8,128)S(1)}, u32[]{:S(2)}, u32[]{:S(2)}) async-start(f32[8,3,8,512]{3,2,1,0:T(8,128)} %reshape.312), calls=%async_computation.2 | async-start | bytes 786432 | tf_op jit(solution)/shard_map/all_to_all | solution.py:393
  79.3 165.9 %all-gather.7.cloned.1.call-start = ((), (), s32[]{:S(2)}) async-start(), calls=%async_computation.8 | async-start | bytes 6684672 | tf_op jit(solution)/shard_map/all_gather | solution.py:398
  92.2 26.5 %copy-start.30 = (pred[5,8,8]{2,1,0:T(8,128)(4,1)S(1)}, pred[5,8,8]{2,1,0:T(8,128)(4,1)}, u32[]{:S(2)}) copy-start(pred[5,8,8]{2,1,0:T(8,128)(4,1)} %constant_dynamic-update-slice_fusion) | copy-start | bytes 964
  92.2 26.7 %copy-start.10 = (f32[64,4,128]{2,1,0:T(4,128)S(1)}, f32[64,4,128]{2,1,0:T(4,128)}, u32[]{:S(2)}) copy-start(f32[64,4,128]{2,1,0:T(4,128)} %copy-done.9) | copy-start | bytes 393220
  92.2 27.4 %copy-start.8 = (f32[64,4,128]{2,1,0:T(4,128)S(1)}, f32[64,4,128]{2,1,0:T(4,128)}, u32[]{:S(2)}) copy-start(f32[64,4,128]{2,1,0:T(4,128)} %copy-done.7) | copy-start | bytes 393220
  92.2 28.0 %copy-start.6 = (f32[64,4,128]{2,1,0:T(4,128)S(1)}, f32[64,4,128]{2,1,0:T(4,128)}, u32[]{:S(2)}) copy-start(f32[64,4,128]{2,1,0:T(4,128)} %copy-done.5) | copy-start | bytes 393220
  120.2 67.7 %all-to-all-start.3 = ((f32[128,8,8,128]{3,2,1,0:T(8,128)}), f32[128,8,8,128]{3,2,1,0:T(8,128)}, u32[]{:S(2)}, u32[]{:S(2)}) async-start(f32[128,8,8,128]{3,2,1,0:T(8,128)} %bitcast.135), calls=%async_computation.3 | async-start | bytes 8388608 | tf_op jit(solution)/shard_map/all_to_all | solution.py:399
  127.2 23.8 %slice-start = ((s8[6291456]{0:T(1024)(128)(4,1)}), s8[4194304]{0:T(1024)(128)(4,1)S(1)}, s32[]{:S(2)}) async-start(s8[6291456]{0:T(1024)(128)(4,1)} %bitcast.147), calls=%async_computation.9 | async-start | bytes 8388608
  128.7 22.4 %slice-start.1 = ((s8[6291456]{0:T(1024)(128)(4,1)}), s8[2097152]{0:T(1024)(128)(4,1)S(1)}, s32[]{:S(2)}) async-start(s8[6291456]{0:T(1024)(128)(4,1)} %bitcast.147), calls=%async_computation.10 | async-start | bytes 4194304
  153.0 30.2 %copy-start.13 = (f32[512,512]{1,0:T(8,128)}, f32[512,512]{1,0:T(8,128)S(1)}, u32[]{:S(2)}) copy-start(f32[512,512]{1,0:T(8,128)S(1)} %fusion.2) | copy-start | bytes 3145732
  154.9 52.9 %copy-start.11 = (f32[512,512]{1,0:T(8,128)}, f32[512,512]{1,0:T(8,128)S(1)}, u32[]{:S(2)}) copy-start(f32[512,512]{1,0:T(8,128)S(1)} %fusion.4) | copy-start | bytes 3145732
  195.7 49.5 %all-to-all-start.4 = ((f32[128,4,8,128]{3,2,1,0:T(8,128)}), f32[128,4,8,128]{3,2,1,0:T(8,128)}, u32[]{:S(2)}, u32[]{:S(2)}) async-start(f32[128,4,8,128]{3,2,1,0:T(8,128)} %bitcast.136), calls=%async_computation.4 | async-start | bytes 4194304 | tf_op jit(solution)/shard_map/all_to_all | solution.py:418
  259.2 34.8 %all-to-all-start.5 = ((f32[128,3,4,256]{3,2,1,0:T(4,128)}), f32[128,3,4,256]{3,2,1,0:T(4,128)}, u32[]{:S(2)}, u32[]{:S(2)}) async-start(f32[128,3,4,256]{3,2,1,0:T(4,128)} %bitcast.152), calls=%async_computation.5 | async-start | bytes 3145728 | tf_op jit(solution)/shard_map/all_to_all | solution.py:359
  296.8 6.9 %collective-permute-start = (f32[128,3,4,256]{3,0,2,1:T(8,128)}, f32[128,3,4,256]{3,0,2,1:T(8,128)}, u32[]{:S(2)}, u32[]{:S(2)}) collective-permute-start(f32[128,3,4,256]{3,0,2,1:T(8,128)} %copy.73), channel_id=1, source_target_pairs={{0,1},{1,0},{2,3},{3,2},{4,5},{5,4},{6,7},{7,6},{8,9},{9,8},{10,11... | collective-permute-start | bytes 4718600 | tf_op jit(solution)/shard_map/ppermute | solution.py:363
  299.9 23.0 %all-to-all-start.6 = ((f32[128,2,4,256]{3,2,1,0:T(4,128)}), f32[128,2,4,256]{3,2,1,0:T(4,128)S(1)}, u32[]{:S(2)}, u32[]{:S(2)}) async-start(f32[128,2,4,256]{3,2,1,0:T(4,128)} %bitcast.154), calls=%async_computation.6 | async-start | bytes 2097152 | tf_op jit(solution)/shard_map/all_to_all | solution.py:359
  322.9 3.5 %collective-permute-start.1 = (f32[128,2,4,256]{3,2,1,0:T(4,128)S(1)}, f32[128,2,4,256]{3,2,1,0:T(4,128)S(1)}, u32[]{:S(2)}, u32[]{:S(2)}) collective-permute-start(f32[128,2,4,256]{3,2,1,0:T(4,128)S(1)} %all-to-all-done.6), channel_id=1, source_target_pairs={{0,1},{1,0},{2,3},{3,2},{4,5},{5,4},{6,7},{7,6},{8,9},{9,8},{10,11... | collective-permute-start | bytes 3145736 | tf_op jit(solution)/shard_map/ppermute | solution.py:363
  (22 other events, 58.4 us)
Sparse Core Ops, SparseCore 0:
  38.2 72.5 all-gather.4
  118.8 116.4 all-gather.6
